TPU v7x, 32 devices: a whole 2x2x4 slice. The times are simulated.
32 devices in a mesh: dp: 16 (over z, y, core), tensor: 2 (over x).
Axes of the slice: x: 2, y: 2, z: 4, core: 2. Of those that a mesh axis runs over, the one named last changes fastest.
Arguments:
- tokens: bfloat16 [16384, 768], P(('dp', 'tensor')), may hold values from -6 to 6
- encoded: bfloat16 [48, 512, 768], P('dp', 'tensor'), may hold values from -6 to 6
- cotangent: bfloat16 [16384, 768], P(('dp', 'tensor')), may hold values from -6 to 6
- segments: int32 [16, 1024], P('dp'), may hold values from 0 to 2, never falling along the last dimension, each value on 1 to 1022 neighbouring positions
- enc_lengths: int32 [48], P('dp'), may hold values from 128 to 512, as said below
- rel_buckets: int32 [1022], replicated, may hold values from 0 to 31, as said below
- gain_self: bfloat16 [768], P('dp'), may hold values from 0.5 to 1.5
- self_query: bfloat16 [768, 768], P('dp', 'tensor'), may hold values from -0.0546875 to 0.0546875
- self_key: bfloat16 [768, 768], P('dp', 'tensor'), may hold values from -0.21875 to 0.21875
- self_value: bfloat16 [768, 768], P('dp', 'tensor'), may hold values from -0.21875 to 0.21875
- self_out: bfloat16 [768, 768], P('dp', 'tensor'), may hold values from -1.25 to 1.25
- rel_table: float32 [32, 12], P(None, 'tensor'), may hold values from -4 to 4
- gain_cross: bfloat16 [768], P('dp'), may hold values from 0.5 to 1.5
- cross_query: bfloat16 [768, 768], P('dp', 'tensor'), may hold values from -0.0546875 to 0.0546875
- cross_key: bfloat16 [768, 768], P('dp', 'tensor'), may hold values from -0.21875 to 0.21875
- cross_value: bfloat16 [768, 768], P('dp', 'tensor'), may hold values from -0.21875 to 0.21875
- cross_out: bfloat16 [768, 768], P('dp', 'tensor'), may hold values from -1.25 to 1.25
- gain_ff: bfloat16 [768], P('dp'), may hold values from 0.5 to 1.5
- ff_gate: bfloat16 [768, 2048], P('dp', 'tensor'), may hold values from -0.21875 to 0.21875
- ff_up: bfloat16 [768, 2048], P('dp', 'tensor'), may hold values from -0.21875 to 0.21875
- ff_down: bfloat16 [768, 2048], P('dp', 'tensor'), may hold values from -0.125 to 0.125
Outputs:
- output: float32 [16384, 768], P(('dp', 'tensor'))
- grad_tokens: float32 [16384, 768], P(('dp', 'tensor'))
- grad_encoded: float32 [48, 512, 768], P('dp', 'tensor')
- grad_gain_self: float32 [768], P('dp')
- grad_self_query: float32 [768, 768], P('dp', 'tensor')
- grad_self_key: float32 [768, 768], P('dp', 'tensor')
- grad_self_value: float32 [768, 768], P('dp', 'tensor')
- grad_self_out: float32 [768, 768], P('dp', 'tensor')
- grad_rel_table: float32 [32, 12], P(None, 'tensor')
- grad_gain_cross: float32 [768], P('dp')
- grad_cross_query: float32 [768, 768], P('dp', 'tensor')
- grad_cross_key: float32 [768, 768], P('dp', 'tensor')
- grad_cross_value: float32 [768, 768], P('dp', 'tensor')
- grad_cross_out: float32 [768, 768], P('dp', 'tensor')
- grad_gain_ff: float32 [768], P('dp')
- grad_ff_gate: float32 [768, 2048], P('dp', 'tensor')
- grad_ff_up: float32 [768, 2048], P('dp', 'tensor')
- grad_ff_down: float32 [768, 2048], P('dp', 'tensor')
Inputs may be any that keep to these rules, and one draw needn't show every extreme that they name: `segments`: sequence numbers never fall along a group, every number of 0 to 2 occurs, and no sequence has more than 1022 tokens; sequence s of group g reads encoder sequence g * 3 + s. `enc_lengths`: the live encoder tokens are the first ones of their sequence. rel_buckets[n] = n for n below 16; beyond that it never falls and rises by at most one from n to n + 1.
All inputs are finite; a program needn't handle non-finite values.
Results may differ from a plain program's by a relative error of at most 0.033.
Values may be sent and summed in bfloat16 or wider, within the bound.
No kernel may reach another device: no remote copies, remote signals or barrier semaphores. Data moves between devices by JAX's collectives and lax.ppermute only.
A program may use at most 384 MiB of HBM per device.

v0:
```python
import jax
import jax.numpy as jnp
from jax import lax
from jax.sharding import PartitionSpec as P

epsilon = 1e-06
masked_out = -1000000000.0


def normalize(vector, gain_row):
    scaling = lax.rsqrt(jnp.mean(vector * vector, axis=1, keepdims=True) + epsilon)
    normed = vector * scaling
    return (normed, scaling, (normed * gain_row.astype(jnp.float32)).astype(jnp.bfloat16))


def norm_back(upstream, normed, scaling, gain_row):
    direct = upstream * gain_row.astype(jnp.float32)
    inner = jnp.mean(direct * normed, axis=1, keepdims=True)
    return (scaling * (direct - normed * inner), jnp.sum(upstream * normed, axis=0))


def product(left, right):
    return jnp.dot(left, right, preferred_element_type=jnp.float32)


def product_nt(left, right):
    return lax.dot_general(
        left, right, (((1,), (1,)), ((), ())), preferred_element_type=jnp.float32
    )


def product_tn(left, right):
    return lax.dot_general(
        left, right, (((0,), (0,)), ((), ())), preferred_element_type=jnp.float32
    )


def block_scores(queries, key3, extras, start_row, block_rows, head_count, head_size):
    part = queries[start_row : start_row + block_rows].reshape(block_rows, head_count, head_size)
    scores = jnp.einsum("qhd,khd->hqk", part, key3, preferred_element_type=jnp.float32)
    bias_of, allowed = extras(start_row, block_rows)
    return (jnp.where(allowed[None], scores + bias_of, masked_out), part)


def attend_forward(queries, key_rows, value_rows, extras, head_size, block_rows):
    head_count = queries.shape[1] // head_size
    key3 = key_rows.reshape(key_rows.shape[0], head_count, head_size)
    value3 = value_rows.reshape(value_rows.shape[0], head_count, head_size)
    outputs = []
    log_sums = []
    for start_row in range(0, queries.shape[0], block_rows):
        scores, part = block_scores(
            queries, key3, extras, start_row, block_rows, head_count, head_size
        )
        row_max = jnp.max(scores, axis=2, keepdims=True)
        exponent = jnp.exp(scores - row_max)
        row_sum = jnp.sum(exponent, axis=2, keepdims=True)
        softened = (exponent / row_sum).astype(jnp.bfloat16)
        mixture = jnp.einsum("hqk,khd->qhd", softened, value3, preferred_element_type=jnp.float32)
        outputs.append(mixture.reshape(block_rows, head_count * head_size).astype(jnp.bfloat16))
        log_sums.append(row_max + jnp.log(row_sum))
    return (jnp.concatenate(outputs, axis=0), log_sums)


def attend_backward(
    queries, key_rows, value_rows, grad_out, log_sums, extras, bias_grad, head_size, block_rows
):
    head_count = queries.shape[1] // head_size
    key3 = key_rows.reshape(key_rows.shape[0], head_count, head_size)
    value3 = value_rows.reshape(value_rows.shape[0], head_count, head_size)
    d_keys = jnp.zeros(key3.shape, jnp.float32)
    d_values = jnp.zeros(value3.shape, jnp.float32)
    d_queries = []
    bias_total = jnp.float32(0.0)
    for block_index, start_row in enumerate(range(0, queries.shape[0], block_rows)):
        scores, part = block_scores(
            queries, key3, extras, start_row, block_rows, head_count, head_size
        )
        softened = jnp.exp(scores - log_sums[block_index])
        grad_part = grad_out[start_row : start_row + block_rows].reshape(
            block_rows, head_count, head_size
        )
        d_soft = jnp.einsum("qhd,khd->hqk", grad_part, value3, preferred_element_type=jnp.float32)
        inner = jnp.sum(softened * d_soft, axis=2, keepdims=True)
        d_scores = (softened * (d_soft - inner)).astype(jnp.bfloat16)
        d_part = jnp.einsum("hqk,khd->qhd", d_scores, key3, preferred_element_type=jnp.float32)
        d_queries.append(d_part.reshape(block_rows, head_count * head_size).astype(jnp.bfloat16))
        d_keys = d_keys + jnp.einsum(
            "hqk,qhd->khd", d_scores, part, preferred_element_type=jnp.float32
        )
        d_values = d_values + jnp.einsum(
            "hqk,qhd->khd",
            softened.astype(jnp.bfloat16),
            grad_part,
            preferred_element_type=jnp.float32,
        )
        bias_total = bias_total + bias_grad(start_row, block_rows, d_scores)
    width = head_count * head_size
    return (
        jnp.concatenate(d_queries, axis=0),
        d_keys.reshape(-1, width).astype(jnp.bfloat16),
        d_values.reshape(-1, width).astype(jnp.bfloat16),
        bias_total,
    )


def local(
    tokens,
    encoded,
    cotangent,
    segments,
    enc_lengths,
    rel_buckets,
    gain_self,
    self_query,
    self_key,
    self_value,
    self_out,
    rel_table,
    gain_cross,
    cross_query,
    cross_key,
    cross_value,
    cross_out,
    gain_ff,
    ff_gate,
    ff_up,
    ff_down,
):
    segment = segments[0]
    group_rows = segment.shape[0]
    block_rows = min(512, group_rows)
    span = rel_buckets.shape[0]
    bucket_count = rel_table.shape[0]
    head_local = rel_table.shape[1]
    head_size = self_query.shape[1] // head_local
    enc_len = encoded.shape[1] * lax.axis_size("tensor")
    position = jnp.arange(group_rows, dtype=jnp.int32)
    bucket_ids = jnp.arange(bucket_count + 1, dtype=jnp.int32)
    bucket_first = jnp.sum((rel_buckets[None, :] < bucket_ids[:, None]).astype(jnp.int32), axis=1)
    bucket_first = jnp.where(bucket_ids == bucket_count, span, bucket_first)
    lower_edge = bucket_first[:bucket_count]
    upper_edge = bucket_first[1:]
    table_high = rel_table.astype(jnp.bfloat16)
    rest_one = rel_table - table_high.astype(jnp.float32)
    table_mid = rest_one.astype(jnp.bfloat16)
    table_low = (rest_one - table_mid.astype(jnp.float32)).astype(jnp.bfloat16)
    key_place = jnp.arange(encoded.shape[0] * enc_len, dtype=jnp.int32)
    key_seq = key_place // enc_len
    live = key_place % enc_len < jnp.repeat(
        enc_lengths, enc_len, total_repeat_length=key_place.shape[0]
    )

    def bucket_block(start_row, count):
        rows_here = position[start_row : start_row + count]
        distance = jnp.clip(rows_here[:, None] - position[None, :], 0, span - 1)
        inside = (distance[None] >= lower_edge[:, None, None]) & (
            distance[None] < upper_edge[:, None, None]
        )
        return inside.astype(jnp.bfloat16)

    def self_extras(start_row, count):
        rows_here = position[start_row : start_row + count]
        distance = rows_here[:, None] - position[None, :]
        allowed = (distance >= 0) & (
            segment[start_row : start_row + count][:, None] == segment[None, :]
        )
        selector = bucket_block(start_row, count)
        bias_high = jnp.einsum(
            "ch,cqk->hqk", table_high, selector, preferred_element_type=jnp.float32
        )
        bias_mid = jnp.einsum(
            "ch,cqk->hqk", table_mid, selector, preferred_element_type=jnp.float32
        )
        bias_low = jnp.einsum(
            "ch,cqk->hqk", table_low, selector, preferred_element_type=jnp.float32
        )
        return (bias_high + bias_mid + bias_low, allowed)

    def cross_extras(start_row, count):
        allowed = (segment[start_row : start_row + count][:, None] == key_seq[None, :]) & live[
            None, :
        ]
        return (jnp.float32(0.0), allowed)

    def self_bias_grad(start_row, count, d_scores):
        selector = bucket_block(start_row, count)
        return jnp.einsum("hqk,cqk->ch", d_scores, selector, preferred_element_type=jnp.float32)

    def no_bias_grad(start_row, count, d_scores):
        return jnp.float32(0.0)

    def gather_rows(own_part):
        return lax.all_gather(own_part, "tensor", axis=0, tiled=True)

    def sum_rows(partial_rows):
        return lax.psum_scatter(partial_rows, "tensor", scatter_dimension=0, tiled=True)

    def fetch_attention(gain_row, first_w, second_w, third_w, fourth_w):
        return (
            lax.all_gather(gain_row, "dp", axis=0, tiled=True),
            lax.all_gather(first_w, "dp", axis=0, tiled=True),
            lax.all_gather(second_w, "dp", axis=0, tiled=True),
            lax.all_gather(third_w, "dp", axis=0, tiled=True),
            lax.all_gather(fourth_w, "dp", axis=0, tiled=True),
        )

    def refetch_attention(gain_row, first_w, second_w, third_w, fourth_w):
        return (
            lax.all_gather(gain_row, "dp", axis=0, tiled=True),
            lax.all_gather(first_w, "dp", axis=0, tiled=True),
            lax.all_gather(second_w, "dp", axis=0, tiled=True),
            lax.all_gather(third_w, "dp", axis=0, tiled=True),
            lax.all_gather(fourth_w, "dp", axis=0, tiled=True),
        )

    def reduce_attention(first_g, second_g, third_g, fourth_g):
        return (
            lax.psum_scatter(first_g, "dp", scatter_dimension=0, tiled=True),
            lax.psum_scatter(second_g, "dp", scatter_dimension=0, tiled=True),
            lax.psum_scatter(third_g, "dp", scatter_dimension=0, tiled=True),
            lax.psum_scatter(fourth_g, "dp", scatter_dimension=0, tiled=True),
        )

    inputs = tokens.astype(jnp.float32)
    gain_s, w_query, w_key, w_value, w_out = fetch_attention(
        gain_self, self_query, self_key, self_value, self_out
    )
    normed_one, scale_one, own_one = normalize(inputs, gain_s)
    rows_one = gather_rows(own_one)
    width = w_query.shape[1]
    w_qkv = jnp.concatenate((w_query, w_key, w_value), axis=1)
    qkv = product(rows_one, w_qkv).astype(jnp.bfloat16)
    query_s, key_s, value_s = (qkv[:, :width], qkv[:, width : 2 * width], qkv[:, 2 * width :])
    attended, sums_self = attend_forward(
        query_s, key_s, value_s, self_extras, head_size, block_rows
    )
    hidden_one = inputs + sum_rows(product_nt(attended, w_out))
    gain_c, c_query, c_key, c_value, c_out = fetch_attention(
        gain_cross, cross_query, cross_key, cross_value, cross_out
    )
    normed_two, scale_two, own_two = normalize(hidden_one, gain_c)
    rows_two = gather_rows(own_two)
    query_c = product(rows_two, c_query).astype(jnp.bfloat16)
    states = lax.all_gather(encoded, "tensor", axis=1, tiled=True).reshape(-1, encoded.shape[2])
    w_kv = jnp.concatenate((c_key, c_value), axis=1)
    key_value = product(states, w_kv).astype(jnp.bfloat16)
    key_c, value_c = (key_value[:, :width], key_value[:, width:])
    crossed, sums_cross = attend_forward(
        query_c, key_c, value_c, cross_extras, head_size, block_rows
    )
    hidden_two = hidden_one + sum_rows(product_nt(crossed, c_out))
    gain_f, w_gate, w_up, w_down = (
        lax.all_gather(gain_ff, "dp", axis=0, tiled=True),
        lax.all_gather(ff_gate, "dp", axis=0, tiled=True),
        lax.all_gather(ff_up, "dp", axis=0, tiled=True),
        lax.all_gather(ff_down, "dp", axis=0, tiled=True),
    )
    normed_three, scale_three, own_three = normalize(hidden_two, gain_f)
    rows_three = gather_rows(own_three)
    hidden_width = w_gate.shape[1]
    w_gate_up = jnp.concatenate((w_gate, w_up), axis=1)
    gate_up = product(rows_three, w_gate_up).astype(jnp.bfloat16)
    gate_part, up_part = (gate_up[:, :hidden_width], gate_up[:, hidden_width:])
    activated, gelu_pull = jax.vjp(
        lambda gate_in: jax.nn.gelu(gate_in, approximate=True), gate_part.astype(jnp.float32)
    )
    up_float = up_part.astype(jnp.float32)
    hidden = (activated * up_float).astype(jnp.bfloat16)
    output = hidden_two + sum_rows(product_nt(hidden, w_down))
    gain_f, w_gate, w_up, w_down = (
        lax.all_gather(gain_ff, "dp", axis=0, tiled=True),
        lax.all_gather(ff_gate, "dp", axis=0, tiled=True),
        lax.all_gather(ff_up, "dp", axis=0, tiled=True),
        lax.all_gather(ff_down, "dp", axis=0, tiled=True),
    )
    w_gate_up = jnp.concatenate((w_gate, w_up), axis=1)
    d_output = cotangent.astype(jnp.float32)
    d_branch = gather_rows(cotangent)
    d_down = product_tn(d_branch, hidden)
    d_hidden = product(d_branch, w_down)
    (d_gate,) = gelu_pull(d_hidden * up_float)
    d_up = d_hidden * activated
    d_gate_up = jnp.concatenate((d_gate, d_up), axis=1).astype(jnp.bfloat16)
    d_w_gate_up = product_tn(rows_three, d_gate_up)
    d_ff_gate, d_ff_up = (d_w_gate_up[:, :hidden_width], d_w_gate_up[:, hidden_width:])
    d_normed_three = sum_rows(product_nt(d_gate_up, w_gate_up))
    d_through, d_gain_f = norm_back(d_normed_three, normed_three, scale_three, gain_f)
    d_hidden_two = d_output + d_through
    grads_ff = (
        lax.psum_scatter(d_ff_gate, "dp", scatter_dimension=0, tiled=True),
        lax.psum_scatter(d_ff_up, "dp", scatter_dimension=0, tiled=True),
        lax.psum_scatter(d_down, "dp", scatter_dimension=0, tiled=True),
    )
    gain_c, c_query, c_key, c_value, c_out = refetch_attention(
        gain_cross, cross_query, cross_key, cross_value, cross_out
    )
    w_kv = jnp.concatenate((c_key, c_value), axis=1)
    d_branch_two = gather_rows(d_hidden_two.astype(jnp.bfloat16))
    d_c_out = product_tn(d_branch_two, crossed)
    d_crossed = product(d_branch_two, c_out).astype(jnp.bfloat16)
    d_query_c, d_key_c, d_value_c, unused_bias = attend_backward(
        query_c,
        key_c,
        value_c,
        d_crossed,
        sums_cross,
        cross_extras,
        no_bias_grad,
        head_size,
        block_rows,
    )
    d_c_query = product_tn(rows_two, d_query_c)
    d_key_value = jnp.concatenate((d_key_c, d_value_c), axis=1)
    d_w_kv = product_tn(states, d_key_value)
    d_c_key, d_c_value = (d_w_kv[:, :width], d_w_kv[:, width:])
    d_states = product_nt(d_key_value, w_kv).reshape(encoded.shape[0], enc_len, encoded.shape[2])
    grad_encoded = lax.psum_scatter(d_states, "tensor", scatter_dimension=1, tiled=True)
    d_normed_two = sum_rows(product_nt(d_query_c, c_query))
    d_through_two, d_gain_c = norm_back(d_normed_two, normed_two, scale_two, gain_c)
    d_hidden_one = d_hidden_two + d_through_two
    grads_cross = reduce_attention(d_c_query, d_c_key, d_c_value, d_c_out)
    gain_s, w_query, w_key, w_value, w_out = refetch_attention(
        gain_self, self_query, self_key, self_value, self_out
    )
    w_qkv = jnp.concatenate((w_query, w_key, w_value), axis=1)
    d_branch_one = gather_rows(d_hidden_one.astype(jnp.bfloat16))
    d_s_out = product_tn(d_branch_one, attended)
    d_attended = product(d_branch_one, w_out).astype(jnp.bfloat16)
    d_query_s, d_key_s, d_value_s, d_table = attend_backward(
        query_s,
        key_s,
        value_s,
        d_attended,
        sums_self,
        self_extras,
        self_bias_grad,
        head_size,
        block_rows,
    )
    d_qkv = jnp.concatenate((d_query_s, d_key_s, d_value_s), axis=1)
    d_w_qkv = product_tn(rows_one, d_qkv)
    d_s_query, d_s_key, d_s_value = (
        d_w_qkv[:, :width],
        d_w_qkv[:, width : 2 * width],
        d_w_qkv[:, 2 * width :],
    )
    d_normed_one = sum_rows(product_nt(d_qkv, w_qkv))
    d_through_one, d_gain_s = norm_back(d_normed_one, normed_one, scale_one, gain_s)
    grad_tokens = d_hidden_one + d_through_one
    grads_self = reduce_attention(d_s_query, d_s_key, d_s_value, d_s_out)
    tensor_at = lax.axis_index("tensor")
    blank = jnp.zeros_like(d_table)
    wide_table = jnp.where(
        tensor_at == 0,
        jnp.concatenate((d_table, blank), axis=1),
        jnp.concatenate((blank, d_table), axis=1),
    )
    sum_gain_s, sum_gain_c, sum_gain_f, sum_table = lax.psum(
        (d_gain_s, d_gain_c, d_gain_f, wide_table), ("dp", "tensor")
    )
    piece = gain_self.shape[0]
    offset = lax.axis_index("dp") * piece
    grad_gain_self = lax.dynamic_slice_in_dim(sum_gain_s, offset, piece)
    grad_gain_cross = lax.dynamic_slice_in_dim(sum_gain_c, offset, piece)
    grad_gain_ff = lax.dynamic_slice_in_dim(sum_gain_f, offset, piece)
    grad_table = lax.dynamic_slice_in_dim(sum_table, tensor_at * head_local, head_local, axis=1)
    return (
        output,
        grad_tokens,
        grad_encoded,
        grad_gain_self,
        grads_self[0],
        grads_self[1],
        grads_self[2],
        grads_self[3],
        grad_table,
        grad_gain_cross,
        grads_cross[0],
        grads_cross[1],
        grads_cross[2],
        grads_cross[3],
        grad_gain_ff,
        grads_ff[0],
        grads_ff[1],
        grads_ff[2],
    )


def solution(mesh):
    in_specs = (
        P(("dp", "tensor"), None),
        P("dp", "tensor", None),
        P(("dp", "tensor"), None),
        P("dp", None),
        P("dp"),
        P(),
        P("dp"),
        P("dp", "tensor"),
        P("dp", "tensor"),
        P("dp", "tensor"),
        P("dp", "tensor"),
        P(None, "tensor"),
        P("dp"),
        P("dp", "tensor"),
        P("dp", "tensor"),
        P("dp", "tensor"),
        P("dp", "tensor"),
        P("dp"),
        P("dp", "tensor"),
        P("dp", "tensor"),
        P("dp", "tensor"),
    )
    out_specs = (
        P(("dp", "tensor"), None),
        P(("dp", "tensor"), None),
        P("dp", "tensor", None),
        P("dp"),
        P("dp", "tensor"),
        P("dp", "tensor"),
        P("dp", "tensor"),
        P("dp", "tensor"),
        P(None, "tensor"),
        P("dp"),
        P("dp", "tensor"),
        P("dp", "tensor"),
        P("dp", "tensor"),
        P("dp", "tensor"),
        P("dp"),
        P("dp", "tensor"),
        P("dp", "tensor"),
        P("dp", "tensor"),
    )
    return jax.shard_map(local, mesh=mesh, in_specs=in_specs, out_specs=out_specs, check_vma=False)
```

profile of v0, /device:TPU:0, one launch (start us, length us, event | category | flops | bytes accessed | tf_op | source)
XLA Modules:
  0.0 2072.9 jit_solution(14355120027814424998)
XLA Ops:
  13.9 36.0 %all-reduce.6 = (bf16[768]{0:T(1024)(128)(2,1)S(1)}, bf16[768]{0:T(1024)(128)(2,1)}, bf16[768]{0:T(1024)(128)(2,1)}) all-reduce(bf16[768]{0:T(1024)(128)(2,1)S(1)} %dynamic-update-slice.3, bf16[768]{0:T(1024)(128)(2,1)S(1)} %dynamic-update-slice.4, bf16[768]{0:T(1024)(128)(2,1)S(1)} %dynamic-update-slice.5), channel_id=1, replica_groups=mesh['dp'=16,'tensor'=2] {'dp'}, use_global_device_ids=true, to_apply=%add.2 | all-reduce | flops 2304 | bytes 9216
  58.2 29.9 %compare_and_fusion.1 = (pred[32,512,1024]{1,0,2:T(32,128)(4,1)}, pred[32,512,1024]{1,0,2:T(32,128)(4,1)}) fusion(s32[512,1024]{0,1:T(8,128)} %copy.123, s32[32]{0:T(128)S(1)} %get-tuple-element.155, s32[32]{0:T(128)S(1)} %get-tuple-element.154, s32[512,1024]{0,1:T(8,128)} %copy.130), kind=kLoop, calls=%fused_computation.1 | loop fusion | flops 100663296 | bytes 37748992 | tf_op jit(solution)/shard_map/and | solution.py:157
  88.2 90.0 %copy.132 = pred[32,512,1024]{2,0,1:T(32,128)(4,1)} copy(pred[32,512,1024]{1,0,2:T(32,128)(4,1)} %get-tuple-element.150) | data formatting | bytes 33554432 | tf_op jit(solution)/shard_map/and | solution.py:157
  178.2 15.6 fusion.98
  193.7 15.4 fusion.102
  209.2 90.2 %copy.125 = pred[32,512,1024]{2,0,1:T(32,128)(4,1)} copy(pred[32,512,1024]{1,0,2:T(32,128)(4,1)} %get-tuple-element.149) | data formatting | bytes 33554432 | tf_op jit(solution)/shard_map/and | solution.py:157
  299.4 15.4 fusion.107
  314.8 15.5 fusion.106
  330.3 18.9 all_gather.79
  349.2 21.1 %all_gather.80 = bf16[768,384]{1,0:T(8,128)(2,1)S(1)} all-gather(bf16[48,384]{1,0:T(8,128)(2,1)S(1)} %copy-done.88), channel_id=1, replica_groups=mesh['dp'=16,'tensor'=2] {'dp'}, dimensions={0}, use_global_device_ids=true | all-gather | bytes 626688 | tf_op jit(solution)/shard_map/all_gather | solution.py:203
  370.3 19.0 all_gather.81
  389.4 15.7 copy.124
  405.1 15.7 copy.131
  422.4 21.8 %all_gather.82 = bf16[768,384]{1,0:T(8,128)(2,1)} all-gather(bf16[48,384]{1,0:T(8,128)(2,1)S(1)} %copy-done.90), channel_id=1, replica_groups=mesh['dp'=16,'tensor'=2] {'dp'}, dimensions={0}, use_global_device_ids=true | all-gather | bytes 626688 | tf_op jit(solution)/shard_map/all_gather | solution.py:205
  444.3 15.8 fusion.100
  460.1 15.4 fusion.104
  484.4 31.3 %fusion.142 = (f32[6,512]{1,0:T(8,128)S(1)}, f32[6,512,1024]{2,1,0:T(8,128)}) fusion(f32[6,512,1024]{2,0,1:T(8,128)} %fusion.100, f32[6,512,1024]{2,0,1:T(8,128)} %fusion.104, f32[512,1024,6]{1,0,2:T(8,128)} %copy.124, bf16[512,6,64]{0,2,1:T(8,128)(2,1)S(1)} %bitcast.201, bf16[1024,6,64]{0,2,1:T(8,128)(2,1)S(1)} %bitcast.186, ...), kind=kOutput, calls=%fused_computation.229 | convolution fusion | flops 418378752 | bytes 52047872 | tf_op jit(solution)/shard_map/qhd,khd->hqk/dot_general | solution.py:40
  527.6 31.3 %fusion.141 = (f32[6,512]{1,0:T(8,128)S(1)}, f32[6,512,1024]{2,1,0:T(8,128)}) fusion(f32[6,512,1024]{2,0,1:T(8,128)} %fusion.98, f32[6,512,1024]{2,0,1:T(8,128)} %fusion.102, f32[512,1024,6]{1,0,2:T(8,128)} %copy.131, bf16[512,6,64]{0,2,1:T(8,128)(2,1)S(1)} %bitcast.199, bf16[1024,6,64]{0,2,1:T(8,128)(2,1)S(1)} %bitcast.187, ...), kind=kOutput, calls=%fused_computation.228 | convolution fusion | flops 418378752 | bytes 52047872 | tf_op jit(solution)/shard_map/qhd,khd->hqk/dot_general | solution.py:40
  574.7 19.1 all_gather.83
  593.9 20.4 all_gather.84
  617.3 19.1 all_gather.88
  636.4 21.8 %all_gather.89 = bf16[768,384]{1,0:T(8,128)(2,1)} all-gather(bf16[48,384]{1,0:T(8,128)(2,1)S(1)} %copy-done.94), channel_id=1, replica_groups=mesh['dp'=16,'tensor'=2] {'dp'}, dimensions={0}, use_global_device_ids=true | all-gather | bytes 626688 | tf_op jit(solution)/shard_map/all_gather | solution.py:205
  669.2 16.4 all-gather.15.cloned.1.call-done
  729.1 42.3 %reduce-scatter.27.cloned.1.call-done = f32[512,768]{1,0:T(8,128)} async-done(((f32[1024,768]{1,0:T(8,128)}), f32[512,768]{1,0:T(8,128)}) %reduce-scatter.27.cloned.1.call-update) | async-done | bytes 1572880 | tf_op jit(solution)/shard_map/reduce_scatter | solution.py:197
  779.8 31.2 %all-gather.21.cloned.1.call-done = bf16[768,1024]{1,0:T(8,128)(2,1)} async-done(((bf16[48,1024]{1,0:T(8,128)(2,1)}), bf16[768,1024]{1,0:T(8,128)(2,1)}) %all-gather.21.cloned.1.call-update) | async-done | bytes 1572880 | tf_op jit(solution)/shard_map/all_gather | solution.py:256
  813.8 24.9 %all-gather.17.cloned.1.call-done = bf16[1024,768]{1,0:T(8,128)(2,1)} async-done(((bf16[512,768]{1,0:T(8,128)(2,1)}), bf16[1024,768]{1,0:T(8,128)(2,1)}) %all-gather.17.cloned.1.call-update) | async-done | bytes 1572880 | tf_op jit(solution)/shard_map/all_gather | solution.py:194
  846.6 20.8 %all-gather.25.cloned.1.call-done = bf16[1024,768]{1,0:T(8,128)(2,1)} async-done(((bf16[512,768]{1,0:T(8,128)(2,1)}), bf16[1024,768]{1,0:T(8,128)(2,1)}) %all-gather.25.cloned.1.call-update) | async-done | bytes 1572880 | tf_op jit(solution)/shard_map/all_gather | solution.py:194
  867.4 42.1 %all-gather.23.cloned.1.call-done = bf16[768,1024]{1,0:T(8,128)(2,1)} async-done(((bf16[48,1024]{1,0:T(8,128)(2,1)}), bf16[768,1024]{1,0:T(8,128)(2,1)}) %all-gather.23.cloned.1.call-update) | async-done | bytes 1572880 | tf_op jit(solution)/shard_map/all_gather | solution.py:257
  924.4 42.0 %reduce-scatter.31.cloned.1.call-done = f32[512,768]{1,0:T(8,128)} async-done(((f32[1024,768]{1,0:T(8,128)}), f32[512,768]{1,0:T(8,128)}) %reduce-scatter.31.cloned.1.call-update) | async-done | bytes 1572880 | tf_op jit(solution)/shard_map/reduce_scatter | solution.py:197
  972.8 26.9 %all-gather.27.cloned.1.call-done = bf16[1024,768]{1,0:T(8,128)(2,1)} async-done(((bf16[512,768]{1,0:T(8,128)(2,1)}), bf16[1024,768]{1,0:T(8,128)(2,1)}) %all-gather.27.cloned.1.call-update) | async-done | bytes 1572880 | tf_op jit(solution)/shard_map/all_gather | solution.py:194
  1002.0 13.9 multiply_reduce_fusion.1
  1015.9 13.3 multiply_reduce_fusion
  1029.3 29.1 %multiply_convert_fusion = (bf16[6,512,1536]{2,1,0:T(8,128)(2,1)S(1)}, bf16[6,512,1536]{2,1,0:T(8,128)(2,1)}) fusion(f32[6,512,1536]{2,1,0:T(8,128)} %get-tuple-element.165, f32[6,512,1536]{2,1,0:T(8,128)} %copy-done.1, f32[6,512]{1,0:T(8,128)S(1)} %get-tuple-element.164, f32[6,512]{1,0:T(8,128)S(1)} %log_add_fusion.2, ...), kind=kLoop, calls=%fused_computation.2 | loop fusion | flops 47185920 | bytes 95993856 | tf_op jit(solution)/shard_map/convert_element_type | solution.py:85
  1080.2 35.7 %reduce-scatter.33.cloned.1.call-done = f32[512,768]{1,0:T(8,128)} async-done(((f32[1024,768]{1,0:T(8,128)}), f32[512,768]{1,0:T(8,128)}) %reduce-scatter.33.cloned.1.call-update) | async-done | bytes 1572880 | tf_op jit(solution)/shard_map/reduce_scatter | solution.py:197
  1118.5 42.8 %reduce-scatter.29.cloned.1.call-done = f32[512,768]{1,0:T(8,128)} async-done(((f32[1024,768]{1,0:T(8,128)}), f32[512,768]{1,0:T(8,128)}) %reduce-scatter.29.cloned.1.call-update) | async-done | bytes 1572880 | tf_op jit(solution)/shard_map/reduce_scatter | solution.py:197
  1167.1 27.2 %all-gather.29.cloned.1.call-done = bf16[1024,768]{1,0:T(8,128)(2,1)} async-done(((bf16[512,768]{1,0:T(8,128)(2,1)}), bf16[1024,768]{1,0:T(8,128)(2,1)}) %all-gather.29.cloned.1.call-update) | async-done | bytes 1572880 | tf_op jit(solution)/shard_map/all_gather | solution.py:194
  1372.4 13.0 fusion.78
  1387.5 41.0 %all-reduce.5 = (f32[768]{0:T(1024)S(1)}, f32[32,12]{0,1:T(8,128)S(1)}, f32[768]{0:T(1024)S(1)}, f32[768]{0:T(1024)S(1)}) all-reduce(f32[768]{0:T(1024)S(1)} %get-tuple-element.106, f32[32,12]{0,1:T(8,128)S(1)} %pad_select_fusion, f32[768]{0:T(1024)S(1)} %copy-done.100, ...), channel_id=1, replica_groups=mesh['dp'=16,'tensor'=2] {'dp','tensor'}, use_global_device_ids=true, to_apply=%region_27.28 | all-reduce | flops 2688 | bytes 21504 | tf_op jit(solution)/shard_map/psum | solution.py:359
  1441.6 69.6 %reduce-scatter.51.cloned.1.call-done = f32[48,1024]{1,0:T(8,128)} async-done(((f32[768,1024]{1,0:T(8,128)}), f32[48,1024]{1,0:T(8,128)}) %reduce-scatter.51.cloned.1.call-update) | async-done | bytes 196624 | tf_op jit(solution)/shard_map/reduce_scatter | solution.py:291
  1511.2 61.1 %reduce-scatter.49.cloned.1.call-done = f32[48,384]{1,0:T(8,128)} async-done(((f32[768,384]{1,0:T(8,128)}), f32[48,384]{1,0:T(8,128)}) %reduce-scatter.49.cloned.1.call-update) | async-done | bytes 73744 | tf_op jit(solution)/shard_map/reduce_scatter | solution.py:222
  1572.3 61.3 %reduce-scatter.57.cloned.1.call-done = f32[48,384]{1,0:T(8,128)} async-done(((f32[768,384]{1,0:T(8,128)}), f32[48,384]{1,0:T(8,128)}) %reduce-scatter.57.cloned.1.call-update) | async-done | bytes 73744
  1633.6 61.1 %reduce-scatter.47.cloned.1.call-done = f32[48,384]{1,0:T(8,128)} async-done(((f32[768,384]{1,0:T(8,128)}), f32[48,384]{1,0:T(8,128)}) %reduce-scatter.47.cloned.1.call-update) | async-done | bytes 73744 | tf_op jit(solution)/shard_map/reduce_scatter | solution.py:219
  1694.7 61.2 %reduce-scatter.55.cloned.1.call-done = f32[48,384]{1,0:T(8,128)} async-done(((f32[768,384]{1,0:T(8,128)}), f32[48,384]{1,0:T(8,128)}) %reduce-scatter.55.cloned.1.call-update) | async-done | bytes 73744
  1755.9 61.7 %reduce-scatter.37.cloned.1.call-done = f32[3,256,768]{2,1,0:T(8,128)} async-done(((f32[3,512,768]{2,1,0:T(8,128)}), f32[3,256,768]{2,1,0:T(8,128)}) %reduce-scatter.37.cloned.1.call-update) | async-done | bytes 2359312 | tf_op jit(solution)/shard_map/reduce_scatter | solution.py:318
  1817.6 62.6 %reduce-scatter.45.cloned.1.call-done = f32[48,384]{1,0:T(8,128)} async-done(((f32[768,384]{1,0:T(8,128)}), f32[48,384]{1,0:T(8,128)}) %reduce-scatter.45.cloned.1.call-update) | async-done | bytes 73744 | tf_op jit(solution)/shard_map/reduce_scatter | solution.py:222
  1880.2 61.6 %reduce-scatter.43.cloned.1.call-done = f32[48,384]{1,0:T(8,128)} async-done(((f32[768,384]{1,0:T(8,128)}), f32[48,384]{1,0:T(8,128)}) %reduce-scatter.43.cloned.1.call-update) | async-done | bytes 73744 | tf_op jit(solution)/shard_map/reduce_scatter | solution.py:221
  1941.8 61.7 %reduce-scatter.41.cloned.1.call-done = f32[48,384]{1,0:T(8,128)} async-done(((f32[768,384]{1,0:T(8,128)}), f32[48,384]{1,0:T(8,128)}) %reduce-scatter.41.cloned.1.call-update) | async-done | bytes 73744 | tf_op jit(solution)/shard_map/reduce_scatter | solution.py:220
  2003.5 61.6 %reduce-scatter.39.cloned.1.call-done = f32[48,384]{1,0:T(8,128)} async-done(((f32[768,384]{1,0:T(8,128)}), f32[48,384]{1,0:T(8,128)}) %reduce-scatter.39.cloned.1.call-update) | async-done | bytes 73744 | tf_op jit(solution)/shard_map/reduce_scatter | solution.py:219
  (426 shorter events, 373.9 us)
Async XLA Ops:
  8.0 467.5 %all-gather.11.cloned.1.call-start = ((), (), s32[]{:S(2)}) async-start(), calls=%async_computation.18 | async-start | bytes 2359296 | tf_op jit(solution)/shard_map/all_gather | solution.py:194
  52.8 605.4 %reduce-scatter.25.cloned.1.call-start = ((), (), s32[]{:S(2)}) async-start(), calls=%async_computation.19 | async-start | bytes 4718592 | tf_op jit(solution)/shard_map/reduce_scatter | solution.py:197
  88.1 90.0 %copy-start.78 = (f32[32,6]{0,1:T(8,128)S(1)}, f32[32,6]{0,1:T(8,128)}, u32[]{:S(2)}) copy-start(f32[32,6]{0,1:T(8,128)} %param.34) | copy-start | bytes 2308
  314.8 55.5 %copy-start.89 = (bf16[48,384]{1,0:T(8,128)(2,1)S(1)}, bf16[48,384]{1,0:T(8,128)(2,1)}, u32[]{:S(2)}) copy-start(bf16[48,384]{1,0:T(8,128)(2,1)} %param.32) | copy-start | bytes 110596
  421.0 54.5 %copy-start.72 = (bf16[768,1152]{1,0:T(8,128)(2,1)}, bf16[768,1152]{1,0:T(8,128)(2,1)S(1)}, u32[]{:S(2)}) copy-start(bf16[768,1152]{1,0:T(8,128)(2,1)S(1)} %constant_dynamic-update-slice_fusion) | copy-start | bytes 5308420
  481.3 46.3 %copy-start.18 = (bf16[1024,384]{0,1:T(8,128)(2,1)}, bf16[1024,384]{0,1:T(8,128)(2,1)S(1)}, u32[]{:S(2)}) copy-start(bf16[1024,384]{0,1:T(8,128)(2,1)S(1)} %copy.122) | copy-start | bytes 2359300
  482.9 44.7 %copy-start.27 = (bf16[512,384]{0,1:T(8,128)(2,1)}, bf16[512,384]{0,1:T(8,128)(2,1)S(1)}, u32[]{:S(2)}) copy-start(bf16[512,384]{0,1:T(8,128)(2,1)S(1)} %copy.129) | copy-start | bytes 1179652
  484.4 82.5 %copy-start.22 = (bf16[1024,384]{0,1:T(8,128)(2,1)}, bf16[1024,384]{0,1:T(8,128)(2,1)S(1)}, u32[]{:S(2)}) copy-start(bf16[1024,384]{0,1:T(8,128)(2,1)S(1)} %copy.120) | copy-start | bytes 2359300
  573.2 63.1 %copy-start.94 = (bf16[48,384]{1,0:T(8,128)(2,1)S(1)}, bf16[48,384]{1,0:T(8,128)(2,1)}, u32[]{:S(2)}) copy-start(bf16[48,384]{1,0:T(8,128)(2,1)} %param.39) | copy-start | bytes 110596
  573.3 84.9 %copy-start.16 = (bf16[512,768]{1,0:T(8,128)(2,1)S(1)}, bf16[512,768]{1,0:T(8,128)(2,1)}, u32[]{:S(2)}) copy-start(bf16[512,768]{1,0:T(8,128)(2,1)} %param.23) | copy-start | bytes 2359300
  573.3 90.0 %all-gather.13.cloned.1.call-start = ((), (), s32[]{:S(2)}) async-start(), calls=%async_computation.20 | async-start | bytes 3538944 | tf_op jit(solution)/shard_map/all_gather | solution.py:245
  574.0 111.6 %all-gather.15.cloned.1.call-start = ((), (), s32[]{:S(2)}) async-start(), calls=%async_computation.21 | async-start | bytes 2359296 | tf_op jit(solution)/shard_map/all_gather | solution.py:194
  574.7 85.2 %copy-start.79 = (f32[768]{0:T(1024)}, f32[768]{0:T(1024)S(1)}, u32[]{:S(2)}) copy-start(f32[768]{0:T(1024)S(1)} %convert_element_type.252) | copy-start | bytes 9220
  636.4 49.3 %copy-start.42 = (bf16[768,384]{1,0:T(8,128)(2,1)}, bf16[768,384]{1,0:T(8,128)(2,1)S(1)}, u32[]{:S(2)}) copy-start(bf16[768,384]{1,0:T(8,128)(2,1)S(1)} %all_gather.88) | copy-start | bytes 1769476
  661.0 110.3 %reduce-scatter.27.cloned.1.call-start = ((), (), s32[]{:S(2)}) async-start(), calls=%async_computation.22 | async-start | bytes 4718592 | tf_op jit(solution)/shard_map/reduce_scatter | solution.py:197
  727.9 49.2 %all-gather.19.cloned.1.call-start = ((), (), s32[]{:S(2)}) async-start(), calls=%async_computation.24 | async-start | bytes 1671168 | tf_op jit(solution)/shard_map/all_gather | solution.py:255
  728.4 82.5 %all-gather.21.cloned.1.call-start = ((), (), s32[]{:S(2)}) async-start(), calls=%async_computation.25 | async-start | bytes 1671168 | tf_op jit(solution)/shard_map/all_gather | solution.py:256
  729.0 109.7 %all-gather.17.cloned.1.call-start = ((), (), s32[]{:S(2)}) async-start(), calls=%async_computation.23 | async-start | bytes 2359296 | tf_op jit(solution)/shard_map/all_gather | solution.py:194
  775.3 92.1 %all-gather.25.cloned.1.call-start = ((), (), s32[]{:S(2)}) async-start(), calls=%async_computation.28 | async-start | bytes 2359296 | tf_op jit(solution)/shard_map/all_gather | solution.py:194
  776.0 133.5 %all-gather.23.cloned.1.call-start = ((), (), s32[]{:S(2)}) async-start(), calls=%async_computation.26 | async-start | bytes 1671168 | tf_op jit(solution)/shard_map/all_gather | solution.py:257
  776.8 189.6 %reduce-scatter.31.cloned.1.call-start = ((), (), s32[]{:S(2)}) async-start(), calls=%async_computation.29 | async-start | bytes 4718592 | tf_op jit(solution)/shard_map/reduce_scatter | solution.py:197
  924.3 45.2 %copy-start.24 = (bf16[512,768]{1,0:T(8,128)(2,1)S(1)}, bf16[512,768]{1,0:T(8,128)(2,1)}, u32[]{:S(2)}) copy-start(bf16[512,768]{1,0:T(8,128)(2,1)} %param.25) | copy-start | bytes 2359300
  924.3 75.3 %copy-start.44 = (bf16[768,384]{1,0:T(8,128)(2,1)S(1)}, bf16[768,384]{1,0:T(8,128)(2,1)}, u32[]{:S(2)}) copy-start(bf16[768,384]{1,0:T(8,128)(2,1)} %all_gather.89) | copy-start | bytes 1769476
  924.3 75.3 %all-gather.27.cloned.1.call-start = ((), (), s32[]{:S(2)}) async-start(), calls=%async_computation.30 | async-start | bytes 2359296 | tf_op jit(solution)/shard_map/all_gather | solution.py:194
  972.3 143.7 %reduce-scatter.33.cloned.1.call-start = ((), (), s32[]{:S(2)}) async-start(), calls=%async_computation.31 | async-start | bytes 4718592 | tf_op jit(solution)/shard_map/reduce_scatter | solution.py:197
  972.8 56.5 %copy-start.70 = (f32[6,512]{1,0:T(8,128)}, f32[6,512]{1,0:T(8,128)S(1)}, u32[]{:S(2)}) copy-start(f32[6,512]{1,0:T(8,128)S(1)} %log_add_fusion.2) | copy-start | bytes 36868
  1072.6 88.7 %reduce-scatter.29.cloned.1.call-start = ((), (), s32[]{:S(2)}) async-start(), calls=%async_computation.27 | async-start | bytes 4718592 | tf_op jit(solution)/shard_map/reduce_scatter | solution.py:197
  1080.2 81.2 %copy-start.25 = (bf16[512,768]{1,0:T(8,128)(2,1)S(1)}, bf16[512,768]{1,0:T(8,128)(2,1)}, u32[]{:S(2)}) copy-start(bf16[512,768]{1,0:T(8,128)(2,1)} %param.25) | copy-start | bytes 2359300
  1080.2 114.2 %all-gather.29.cloned.1.call-start = ((), (), s32[]{:S(2)}) async-start(), calls=%async_computation.32 | async-start | bytes 2359296 | tf_op jit(solution)/shard_map/all_gather | solution.py:194
  1118.5 48.6 %copy-start.75 = (f32[6,512]{1,0:T(8,128)S(1)}, f32[6,512]{1,0:T(8,128)}, u32[]{:S(2)}) copy-start(f32[6,512]{1,0:T(8,128)} %copy-done.74) | copy-start | bytes 36868
  1118.5 48.6 %copy-start.82 = (f32[6,512]{1,0:T(8,128)S(1)}, f32[6,512]{1,0:T(8,128)}, u32[]{:S(2)}) copy-start(f32[6,512]{1,0:T(8,128)} %copy-done.81) | copy-start | bytes 36868
  1118.5 48.6 %copy-start.77 = (f32[6,512]{1,0:T(8,128)S(1)}, f32[6,512]{1,0:T(8,128)}, u32[]{:S(2)}) copy-start(f32[6,512]{1,0:T(8,128)} %copy-done.76) | copy-start | bytes 36868
  1118.5 48.6 %copy-start.84 = (f32[6,512]{1,0:T(8,128)S(1)}, f32[6,512]{1,0:T(8,128)}, u32[]{:S(2)}) copy-start(f32[6,512]{1,0:T(8,128)} %copy-done.83) | copy-start | bytes 36868
  1118.5 75.9 %copy-start.41 = (bf16[768,384]{1,0:T(8,128)(2,1)S(1)}, bf16[768,384]{1,0:T(8,128)(2,1)}, u32[]{:S(2)}) copy-start(bf16[768,384]{1,0:T(8,128)(2,1)} %all_gather.82) | copy-start | bytes 1769476
  1167.0 218.5 %reduce-scatter.35.cloned.1.call-start = ((), (), s32[]{:S(2)}) async-start(), calls=%async_computation.33 | async-start | bytes 4718592 | tf_op jit(solution)/shard_map/reduce_scatter | solution.py:197
  1257.9 175.9 %reduce-scatter.59.cloned.1.call-start = ((), (), s32[]{:S(2)}) async-start(), calls=%async_computation.45 | async-start | bytes 3342336
  1265.9 175.6 %reduce-scatter.53.cloned.1.call-start = ((), (), s32[]{:S(2)}) async-start(), calls=%async_computation.42 | async-start | bytes 3342336 | tf_op jit(solution)/shard_map/reduce_scatter | solution.py:292
  1275.6 235.6 %reduce-scatter.51.cloned.1.call-start = ((), (), s32[]{:S(2)}) async-start(), calls=%async_computation.41 | async-start | bytes 3342336 | tf_op jit(solution)/shard_map/reduce_scatter | solution.py:291
  1276.3 296.0 %reduce-scatter.49.cloned.1.call-start = ((), (), s32[]{:S(2)}) async-start(), calls=%async_computation.40 | async-start | bytes 1253376 | tf_op jit(solution)/shard_map/reduce_scatter | solution.py:222
  1300.4 333.2 %reduce-scatter.57.cloned.1.call-start = ((), (), s32[]{:S(2)}) async-start(), calls=%async_computation.44 | async-start | bytes 1253376
  1313.3 381.4 %reduce-scatter.47.cloned.1.call-start = ((), (), s32[]{:S(2)}) async-start(), calls=%async_computation.39 | async-start | bytes 1253376 | tf_op jit(solution)/shard_map/reduce_scatter | solution.py:219
  1317.0 438.9 %reduce-scatter.55.cloned.1.call-start = ((), (), s32[]{:S(2)}) async-start(), calls=%async_computation.43 | async-start | bytes 1253376
  1318.5 499.2 %reduce-scatter.37.cloned.1.call-start = ((), (), s32[]{:S(2)}) async-start(), calls=%async_computation.34 | async-start | bytes 7077888 | tf_op jit(solution)/shard_map/reduce_scatter | solution.py:318
  1324.4 555.8 %reduce-scatter.45.cloned.1.call-start = ((), (), s32[]{:S(2)}) async-start(), calls=%async_computation.38 | async-start | bytes 1253376 | tf_op jit(solution)/shard_map/reduce_scatter | solution.py:222
  1329.0 612.8 %reduce-scatter.43.cloned.1.call-start = ((), (), s32[]{:S(2)}) async-start(), calls=%async_computation.37 | async-start | bytes 1253376 | tf_op jit(solution)/shard_map/reduce_scatter | solution.py:221
  1334.6 668.8 %reduce-scatter.41.cloned.1.call-start = ((), (), s32[]{:S(2)}) async-start(), calls=%async_computation.36 | async-start | bytes 1253376 | tf_op jit(solution)/shard_map/reduce_scatter | solution.py:220
  1335.4 729.7 %reduce-scatter.39.cloned.1.call-start = ((), (), s32[]{:S(2)}) async-start(), calls=%async_computation.35 | async-start | bytes 1253376 | tf_op jit(solution)/shard_map/reduce_scatter | solution.py:219
  1372.4 58.5 %copy-start.26 = (f32[512,768]{1,0:T(8,128)S(1)}, f32[512,768]{1,0:T(8,128)}, u32[]{:S(2)}) copy-start(f32[512,768]{1,0:T(8,128)} %get-tuple-element.116) | copy-start | bytes 4718596
  (97 other events, 1028.7 us)
Sparse Core Ops, SparseCore 0:
  52.9 24.4 all-gather.10
  573.4 40.6 reduce-scatter.24
  615.7 36.0 all-gather.12
  661.1 24.4 all-gather.14
  728.0 43.3 reduce-scatter.26
  972.4 27.2 all-gather.26
  1167.1 27.2 all-gather.28
  1258.0 43.3 reduce-scatter.34
  1305.8 66.1 reduce-scatter.58
  1376.2 65.2 reduce-scatter.52
  1446.0 65.1 reduce-scatter.50
  1515.2 57.0 reduce-scatter.48
  1576.5 57.0 reduce-scatter.56
  1637.7 57.0 reduce-scatter.46
  1698.8 57.0 reduce-scatter.54
  1758.6 58.9 reduce-scatter.36
  1822.1 58.0 reduce-scatter.44
  1884.7 57.0 reduce-scatter.42
  1946.4 57.0 reduce-scatter.40
  2008.0 57.0 reduce-scatter.38
Sparse Core Ops, SparseCore 1:
  730.6 39.7 all-gather.18
  772.5 38.4 all-gather.20
  813.0 25.7 all-gather.16
  840.3 27.0 all-gather.24
  869.7 39.7 all-gather.22
  924.4 41.9 reduce-scatter.30
  1072.7 43.2 reduce-scatter.32
  1118.1 43.2 reduce-scatter.28
where the time goes:
time: 2090 us; the launch traced here: 2070 us
  waiting for transfers between devices  989 us (47%)
  matrix products  403 us (19%)
  local copies, waits for them, and re-layouts  286 us (14%)
  blocking collectives  238 us (11%)
  other arithmetic  136 us (7%)
    and x2, local copies, waits for them, and re-layouts, bucket_block(): (distance[None] >= lower_edge[:, None, None]) & (distance[None] < upper_e...  180 us
    reduce_scatter x6, waiting for transfers between devices, sum_rows(): lax.psum_scatter(partial_rows, 'tensor', scatter_dimension=0, tiled=True)  163 us
    unnamed x31, waiting for transfers between devices  127 us
    reduce_scatter x2, waiting for transfers between devices, reduce_attention(): lax.psum_scatter(fourth_g, 'dp', scatter_dimension=0, tiled=True)  124 us
    reduce_scatter x2, waiting for transfers between devices, reduce_attention(): lax.psum_scatter(first_g, 'dp', scatter_dimension=0, tiled=True)  123 us
    all_gather x6, waiting for transfers between devices, gather_rows(): return lax.all_gather(own_part, 'tensor', axis=0, tiled=True)  116 us
    dot_general x4, matrix products, block_scores(): jnp.einsum('qhd,khd->hqk', part, key3, preferred_element_type=jnp.float32)  71.5 us
    reduce_scatter x1, waiting for transfers between devices, local(): lax.psum_scatter(d_ff_gate, 'dp', scatter_dimension=0, tiled=True)  69.6 us
  transfers between devices with their start and end apart: 28, of which 22 were waited for; matrix products, arithmetic and copies ran while one was open for 25% of the time, Pallas kernels for 0%

commit v1 on v0

v1 whole, which is shorter than its diff:
```python
import functools

import jax
import jax.numpy as jnp
from jax import lax
from jax.experimental import pallas as pl
from jax.experimental.pallas import tpu as pltpu
from jax.sharding import PartitionSpec as P

epsilon = 1e-06
low_score = -1e30
f32 = jnp.float32
bf16 = jnp.bfloat16
exact = lax.Precision.HIGHEST
QB = 256
TB = 128


def nn(left, right):
    return jnp.dot(left, right, preferred_element_type=f32)


def nt(left, right, precision=None):
    return lax.dot_general(
        left, right, (((1,), (1,)), ((), ())), preferred_element_type=f32, precision=precision
    )


def tn(left, right, precision=None):
    return lax.dot_general(
        left, right, (((0,), (0,)), ((), ())), preferred_element_type=f32, precision=precision
    )


def normalize(vector, gain_row):
    scaling = lax.rsqrt(jnp.mean(vector * vector, axis=1, keepdims=True) + epsilon)
    normed = vector * scaling
    return (normed, scaling, (normed * gain_row).astype(bf16))


def norm_back(upstream, normed, scaling, gain_row):
    direct = upstream * gain_row
    inner = jnp.mean(direct * normed, axis=1, keepdims=True)
    return (scaling * (direct - normed * inner), jnp.sum(upstream * normed, axis=0, keepdims=True))


def flipped(value):
    return jnp.transpose(value.astype(f32)).astype(bf16)


def head_only(value, head, size):
    lane = lax.broadcasted_iota(jnp.int32, value.shape, 1)
    return jnp.where(lane // size == head, value, jnp.zeros_like(value))


def toeplitz(bias_row, width):
    return pltpu.roll(
        jnp.broadcast_to(bias_row, (TB, width)), 0, 1, stride=1, stride_axis=0
    )


def self_tiles(query_block, rows):
    first = query_block * QB // TB
    own = [(j * TB, (first - j + 1) * TB, 0) for j in range((query_block + 1) * QB // TB)]
    shift = rows // TB
    peer = [(rows + j * TB, (shift + first - j + 1) * TB, 1) for j in range(rows // TB)]
    return own, peer


def tile_mask(rows_ref, peer, key_row, lanes):
    place = lax.broadcasted_iota(jnp.int32, (TB, QB), 0) + key_row
    low = rows_ref[2 * peer : 2 * peer + 1, lanes]
    high = rows_ref[2 * peer + 1 : 2 * peer + 2, lanes]
    return (place >= low) & (place <= high)


def self_forward_kernel(
    size, rows_ref, bias_ref, q_ref, k_ref, v_ref, o_ref, lse_ref, vt, toe, score, prob, out_t
):
    rows = q_ref.shape[0]
    width = toe.shape[1]
    vt[...] = flipped(v_ref[...])
    for head in range(q_ref.shape[1] // size):
        toe[...] = toeplitz(bias_ref[0, head : head + 1, :], width)
        q_head = head_only(q_ref[...], head, size)
        cols = slice(head * size, (head + 1) * size)
        for block in range(rows // QB):
            lanes = slice(block * QB, (block + 1) * QB)
            q_block = q_head[lanes]
            top = jnp.full((1, QB), low_score, f32)
            groups = self_tiles(block, rows)
            for group in groups:
                for key_row, bias_at, peer in group:
                    raw = nt(k_ref[key_row : key_row + TB, :], q_block)
                    raw = raw + toe[:, bias_at : bias_at + QB]
                    keep = tile_mask(rows_ref, peer, key_row - peer * rows, lanes)
                    raw = jnp.where(keep, raw, low_score)
                    score[key_row : key_row + TB, :] = raw
                    top = jnp.maximum(top, jnp.max(raw, axis=0, keepdims=True))
            total = jnp.zeros((1, QB), f32)
            mixed = jnp.zeros((size, QB), f32)
            for group in groups:
                for key_row, bias_at, peer in group:
                    weight = jnp.exp(score[key_row : key_row + TB, :] - top)
                    total = total + jnp.sum(weight, axis=0, keepdims=True)
                    prob[key_row : key_row + TB, :] = weight.astype(bf16)
                span = slice(group[0][0], group[-1][0] + TB)
                mixed = mixed + nn(vt[cols, span], prob[span, :])
            out_t[cols, lanes] = mixed / total
            lse_ref[0, head : head + 1, lanes] = top + jnp.log(total)
    o_ref[...] = jnp.transpose(out_t[...]).astype(bf16)


def row_products(grad, out, head, size):
    lane = lax.broadcasted_iota(jnp.int32, (8, grad.shape[1]), 1)
    picker = jnp.where(lane // size == head, 1.0, 0.0).astype(f32)
    both = grad.astype(f32) * out.astype(f32)
    return nt(picker, both, exact)[0:1, :]


def self_backward_kernel(
    size, rows_ref, bias_ref, q_ref, k_ref, v_ref, o_ref, g_ref, lse_ref,
    dq_ref, dk_ref, dv_ref, diag_ref,
    kt, toe, prob, grad, diag, dq_t, dk_sum, dv_sum,
):
    rows = q_ref.shape[0]
    width = toe.shape[1]
    kt[...] = flipped(k_ref[...])
    dk_sum[...] = jnp.zeros_like(dk_sum)
    dv_sum[...] = jnp.zeros_like(dv_sum)
    flip = (
        lax.broadcasted_iota(jnp.int32, (TB, TB), 0) + lax.broadcasted_iota(jnp.int32, (TB, TB), 1)
        == TB - 1
    ).astype(f32)
    for head in range(q_ref.shape[1] // size):
        toe[...] = toeplitz(bias_ref[0, head : head + 1, :], width)
        diag[...] = jnp.zeros_like(diag)
        q_head = head_only(q_ref[...], head, size)
        g_head = head_only(g_ref[...], head, size)
        inner = row_products(g_ref[...], o_ref[...], head, size)
        cols = slice(head * size, (head + 1) * size)
        for block in range(rows // QB):
            lanes = slice(block * QB, (block + 1) * QB)
            q_block = q_head[lanes]
            g_block = g_head[lanes]
            lse = lse_ref[0, head : head + 1, lanes]
            inner_block = inner[:, lanes]
            d_query = jnp.zeros((size, QB), f32)
            for group in self_tiles(block, rows):
                for key_row, bias_at, peer in group:
                    key = slice(key_row, key_row + TB)
                    raw = nt(k_ref[key, :], q_block) + toe[:, bias_at : bias_at + QB]
                    keep = tile_mask(rows_ref, peer, key_row - peer * rows, lanes)
                    weight = jnp.where(keep, jnp.exp(raw - lse), 0.0)
                    pull = weight * (nt(v_ref[key, :], g_block) - inner_block)
                    prob[key, :] = weight.astype(bf16)
                    grad[key, :] = pull.astype(bf16)
                    diag[:, bias_at : bias_at + QB] += pull
                span = slice(group[0][0], group[-1][0] + TB)
                dv_sum[span, :] += nn(prob[span, :], g_block)
                dk_sum[span, :] += nn(grad[span, :], q_block)
                d_query = d_query + nn(kt[cols, span], grad[span, :])
            dq_t[cols, lanes] = d_query
        turned = pltpu.roll(
            jnp.dot(flip, diag[...], precision=exact, preferred_element_type=f32),
            0, 1, stride=1, stride_axis=0,
        )
        diag_ref[0, head : head + 1, :] = jnp.sum(turned, axis=0, keepdims=True)
    dq_ref[...] = jnp.transpose(dq_t[...]).astype(bf16)
    dk_ref[...] = dk_sum[...].astype(bf16)
    dv_ref[...] = dv_sum[...].astype(bf16)


def cross_forward_kernel(
    size, flags_ref, seg_ref, q_ref, k_ref, v_ref, o_ref, lse_ref, vt, prob, out_t
):
    rows = q_ref.shape[0]
    sequences = flags_ref.shape[0]
    half = k_ref.shape[0] // (2 * sequences)
    vt[...] = flipped(v_ref[...])
    out_t[...] = jnp.zeros_like(out_t)
    lse_ref[...] = jnp.zeros_like(lse_ref)
    place = lax.broadcasted_iota(jnp.int32, (half, QB), 0)
    for block in range(rows // QB):
        lanes = slice(block * QB, (block + 1) * QB)
        for seq in range(sequences):

            @pl.when(flags_ref[seq, 2 + block] > 0)
            def body(block=block, seq=seq, lanes=lanes):
                mine = seg_ref[0:1, lanes] == seq
                for head in range(q_ref.shape[1] // size):
                    cols = slice(head * size, (head + 1) * size)
                    q_block = head_only(q_ref[lanes, :], head, size)
                    scores = []
                    for part in range(2):
                        start = (part * sequences + seq) * half
                        raw = nt(k_ref[start : start + half, :], q_block)
                        scores.append(jnp.where(place < flags_ref[seq, part], raw, low_score))
                    top = jnp.maximum(
                        jnp.max(scores[0], axis=0, keepdims=True),
                        jnp.max(scores[1], axis=0, keepdims=True),
                    )
                    total = jnp.zeros((1, QB), f32)
                    mixed = jnp.zeros((size, QB), f32)
                    for part in range(2):
                        start = (part * sequences + seq) * half
                        weight = jnp.exp(scores[part] - top)
                        total = total + jnp.sum(weight, axis=0, keepdims=True)
                        mixed = mixed + nn(vt[cols, start : start + half], weight.astype(bf16))
                    out_t[cols, lanes] = jnp.where(mine, mixed / total, out_t[cols, lanes])
                    lse_ref[0, head : head + 1, lanes] = jnp.where(
                        mine, top + jnp.log(total), lse_ref[0, head : head + 1, lanes]
                    )

    o_ref[...] = jnp.transpose(out_t[...]).astype(bf16)


def cross_backward_kernel(
    size, flags_ref, seg_ref, q_ref, k_ref, v_ref, o_ref, g_ref, lse_ref,
    dq_ref, dk_ref, dv_ref, kt, dq_t, dk_sum, dv_sum,
):
    rows = q_ref.shape[0]
    sequences = flags_ref.shape[0]
    half = k_ref.shape[0] // (2 * sequences)
    kt[...] = flipped(k_ref[...])
    dq_t[...] = jnp.zeros_like(dq_t)
    dk_sum[...] = jnp.zeros_like(dk_sum)
    dv_sum[...] = jnp.zeros_like(dv_sum)
    place = lax.broadcasted_iota(jnp.int32, (half, QB), 0)
    for block in range(rows // QB):
        lanes = slice(block * QB, (block + 1) * QB)
        inners = [
            row_products(g_ref[lanes, :], o_ref[lanes, :], head, size)
            for head in range(q_ref.shape[1] // size)
        ]
        for seq in range(sequences):

            @pl.when(flags_ref[seq, 2 + block] > 0)
            def body(block=block, seq=seq, lanes=lanes, inners=inners):
                mine = seg_ref[0:1, lanes] == seq
                for head in range(q_ref.shape[1] // size):
                    cols = slice(head * size, (head + 1) * size)
                    q_block = head_only(q_ref[lanes, :], head, size)
                    g_block = head_only(g_ref[lanes, :], head, size)
                    lse = lse_ref[0, head : head + 1, lanes]
                    for part in range(2):
                        start = (part * sequences + seq) * half
                        key = slice(start, start + half)
                        raw = nt(k_ref[key, :], q_block)
                        keep = (place < flags_ref[seq, part]) & mine
                        weight = jnp.where(keep, jnp.exp(raw - lse), 0.0)
                        pull = weight * (nt(v_ref[key, :], g_block) - inners[head])
                        pull = pull.astype(bf16)
                        dv_sum[key, :] += nn(weight.astype(bf16), g_block)
                        dk_sum[key, :] += nn(pull, q_block)
                        dq_t[cols, lanes] += nn(kt[cols, key], pull)

    dq_ref[...] = jnp.transpose(dq_t[...]).astype(bf16)
    dk_ref[...] = dk_sum[...].astype(bf16)
    dv_ref[...] = dv_sum[...].astype(bf16)


def column_spec(rows):
    return pl.BlockSpec((rows, TB), lambda p: (0, p))


def whole_spec(array):
    return pl.BlockSpec(array.shape, lambda p: (0,) * array.ndim)


def pair_spec(array):
    return pl.BlockSpec((1,) + array.shape[1:], lambda p: (p, 0, 0))


def cost(queries, keys, columns, products):
    return pl.CostEstimate(
        flops=4 * products * queries * keys * columns,
        bytes_accessed=8 * (queries + keys) * columns,
        transcendentals=queries * keys * columns // 64,
    )


params = pltpu.CompilerParams(vmem_limit_bytes=48 * 1024 * 1024)


def self_forward(size, rows_in, bias, q, k, v):
    rows, keys, pairs = q.shape[0], k.shape[0], q.shape[1] // TB
    lse_shape = jax.ShapeDtypeStruct((pairs, 8, rows), f32)
    return pl.pallas_call(
        functools.partial(self_forward_kernel, size),
        name="self_forward",
        grid=(pairs,),
        in_specs=[whole_spec(rows_in), pair_spec(bias), column_spec(rows), column_spec(keys),
                  column_spec(keys)],
        out_specs=[column_spec(rows), pair_spec(lse_shape)],
        out_shape=[jax.ShapeDtypeStruct(q.shape, bf16), lse_shape],
        scratch_shapes=[
            pltpu.VMEM((TB, keys), bf16),
            pltpu.VMEM((TB, bias.shape[2]), f32),
            pltpu.VMEM((keys, QB), f32),
            pltpu.VMEM((keys, QB), bf16),
            pltpu.VMEM((TB, rows), f32),
        ],
        compiler_params=params,
        cost_estimate=cost(rows, keys, q.shape[1], 2),
    )(rows_in, bias, q, k, v)


def self_backward(size, rows_in, bias, q, k, v, o, g, lse):
    rows, keys, pairs = q.shape[0], k.shape[0], q.shape[1] // TB
    diag_shape = jax.ShapeDtypeStruct((pairs, 8, bias.shape[2]), f32)
    return pl.pallas_call(
        functools.partial(self_backward_kernel, size),
        name="self_backward",
        grid=(pairs,),
        in_specs=[whole_spec(rows_in), pair_spec(bias), column_spec(rows), column_spec(keys),
                  column_spec(keys), column_spec(rows), column_spec(rows), pair_spec(lse)],
        out_specs=[column_spec(rows), column_spec(keys), column_spec(keys), pair_spec(diag_shape)],
        out_shape=[jax.ShapeDtypeStruct(q.shape, bf16), jax.ShapeDtypeStruct(k.shape, bf16),
                   jax.ShapeDtypeStruct(v.shape, bf16), diag_shape],
        scratch_shapes=[
            pltpu.VMEM((TB, keys), bf16),
            pltpu.VMEM((TB, bias.shape[2]), f32),
            pltpu.VMEM((keys, QB), bf16),
            pltpu.VMEM((keys, QB), bf16),
            pltpu.VMEM((TB, bias.shape[2]), f32),
            pltpu.VMEM((TB, rows), f32),
            pltpu.VMEM((keys, TB), f32),
            pltpu.VMEM((keys, TB), f32),
        ],
        compiler_params=params,
        cost_estimate=cost(rows, keys, q.shape[1], 5),
    )(rows_in, bias, q, k, v, o, g, lse)


def cross_forward(size, flags, seg, q, k, v):
    rows, keys, pairs = q.shape[0], k.shape[0], q.shape[1] // TB
    lse_shape = jax.ShapeDtypeStruct((pairs, 8, rows), f32)
    return pl.pallas_call(
        functools.partial(cross_forward_kernel, size),
        name="cross_forward",
        grid=(pairs,),
        in_specs=[pl.BlockSpec(memory_space=pltpu.SMEM), whole_spec(seg), column_spec(rows),
                  column_spec(keys), column_spec(keys)],
        out_specs=[column_spec(rows), pair_spec(lse_shape)],
        out_shape=[jax.ShapeDtypeStruct(q.shape, bf16), lse_shape],
        scratch_shapes=[
            pltpu.VMEM((TB, keys), bf16),
            pltpu.VMEM((keys, QB), bf16),
            pltpu.VMEM((TB, rows), f32),
        ],
        compiler_params=params,
        cost_estimate=cost(rows, keys // 3, q.shape[1], 2),
    )(flags, seg, q, k, v)


def cross_backward(size, flags, seg, q, k, v, o, g, lse):
    rows, keys, pairs = q.shape[0], k.shape[0], q.shape[1] // TB
    return pl.pallas_call(
        functools.partial(cross_backward_kernel, size),
        name="cross_backward",
        grid=(pairs,),
        in_specs=[pl.BlockSpec(memory_space=pltpu.SMEM), whole_spec(seg), column_spec(rows),
                  column_spec(keys), column_spec(keys), column_spec(rows), column_spec(rows),
                  pair_spec(lse)],
        out_specs=[column_spec(rows), column_spec(keys), column_spec(keys)],
        out_shape=[jax.ShapeDtypeStruct(q.shape, bf16), jax.ShapeDtypeStruct(k.shape, bf16),
                   jax.ShapeDtypeStruct(v.shape, bf16)],
        scratch_shapes=[
            pltpu.VMEM((TB, keys), bf16),
            pltpu.VMEM((TB, rows), f32),
            pltpu.VMEM((keys, TB), f32),
            pltpu.VMEM((keys, TB), f32),
        ],
        compiler_params=params,
        cost_estimate=cost(rows, keys // 3, q.shape[1], 5),
    )(flags, seg, q, k, v, o, g, lse)


def swap(value, step):
    if step == "x":
        return lax.ppermute(value, "tensor", [(0, 1), (1, 0)])
    count = lax.axis_size("dp")
    return lax.ppermute(value, "dp", [(i, i ^ (1 << step)) for i in range(count)])


def join_blocks(mine, theirs, sizes, bit, rows):
    before = 1
    for size in sizes[:bit]:
        before *= size
    after = rows
    for size in sizes[bit + 1 :]:
        after *= size
    shape = (before, 1, after, mine.shape[-1])
    both = jnp.concatenate((mine.reshape(shape), theirs.reshape(shape)), axis=1)
    return both.reshape(-1, mine.shape[-1])


def gather_weights(shards, paired, order, bits, gate=None):
    rows = shards[0].shape[0]
    widths = [s.shape[1] for s in shards]
    held = [jnp.concatenate(shards, axis=1)] if len(shards) > 1 else list(shards)
    if gate is not None:
        held = list(lax.optimization_barrier((held[0], gate)))[:1]
    sizes = [1] * bits
    split = False
    witness = None
    for index, step in enumerate(order):
        if index == len(order) - 1:
            witness = held[0]
        got = [swap(h, step) for h in held]
        if step == "x":
            cuts = []
            start = 0
            for width in widths:
                cuts.append(slice(start, start + width))
                start += width
            held = [
                jnp.concatenate((held[0][:, c], got[0][:, c]), axis=1) if p else held[0][:, c]
                for c, p in zip(cuts, paired)
            ]
            split = True
        else:
            held = [join_blocks(h, g, sizes, step, rows) for h, g in zip(held, got)]
            sizes[step] = 2
    return held, witness


def add_low(one, two):
    return (one.astype(f32) + two.astype(f32)).astype(bf16)


def scatter_grads(pieces, order, bits, rows):
    summed = [add_low(keep, swap(send, 0)) for keep, send in pieces]
    widths = [s.shape[1] // 2 for s in summed]
    halves = [
        jnp.concatenate([s[:, :w] for s, w in zip(summed, widths)], axis=1),
        jnp.concatenate([s[:, w:] for s, w in zip(summed, widths)], axis=1),
    ]
    sizes = [1] + [2] * (bits - 1)
    for index, step in enumerate(order):
        last = index == len(order) - 1
        plus = (lambda a, b: a.astype(f32) + b.astype(f32)) if last else add_low
        if step == "x":
            halves = [plus(halves[0], swap(halves[1], "x"))]
        else:
            before = 1
            for size in sizes[:step]:
                before *= size
            width = halves[0].shape[-1]
            cut = [h.reshape(before, 2, -1, width) for h in halves]
            got = [swap(c[:, 1].reshape(-1, width), step) for c in cut]
            halves = [plus(c[:, 0].reshape(-1, width), g) for c, g in zip(cut, got)]
            sizes[step] = 1
    total = halves[0]
    outs = []
    start = 0
    for width in widths:
        outs.append(total[:, start : start + width])
        start += width
    return outs


def split_tn(left, right):
    half = left.shape[1] // 2
    return (tn(left[:, :half], right).astype(bf16), tn(left[:, half:], right).astype(bf16))


def local(
    tokens,
    encoded,
    cotangent,
    segments,
    enc_lengths,
    rel_buckets,
    gain_self,
    self_query,
    self_key,
    self_value,
    self_out,
    rel_table,
    gain_cross,
    cross_query,
    cross_key,
    cross_value,
    cross_out,
    gain_ff,
    ff_gate,
    ff_up,
    ff_down,
):
    count = lax.axis_size("dp")
    bits = count.bit_length() - 1
    piece, head_cols = self_query.shape
    width = tokens.shape[1]
    rows = tokens.shape[0]
    head_local = rel_table.shape[1]
    heads = 2 * head_local
    size = head_cols // head_local
    pairs = heads * size // TB
    bucket_count = rel_table.shape[0]
    span = rel_buckets.shape[0]
    sequences, enc_half = encoded.shape[:2]
    dp_at = lax.axis_index("dp")
    tensor_at = lax.axis_index("tensor")
    far = list(range(2, bits))
    near_first = [["x", 1] + far, [1] + far + ["x"], far + ["x", 1]]
    gather_order = [list(reversed(o)) + [0] for o in near_first]

    feature = jnp.arange(width, dtype=jnp.int32)
    block = feature // piece
    mask = jnp.zeros_like(block)
    for bit in range(bits):
        mask = mask + (((block >> (bits - 1 - bit)) & 1) << bit)
    source = (dp_at.astype(jnp.int32) ^ mask) * piece + feature % piece
    shuffle = (feature[:, None] == source[None, :]).astype(bf16)

    def restore(values):
        high = values.astype(bf16)
        low = (values - high.astype(f32)).astype(bf16)
        return nt(high, shuffle) + nt(low, shuffle)

    gain_cols = jnp.pad(
        jnp.stack((gain_self, gain_cross, gain_ff), axis=1), ((0, 0), (0, TB - 3))
    )
    (w_query, gains), _ = gather_weights(
        [self_query, gain_cols], [True, False], gather_order[0], bits
    )
    (w_key,), wit_a = gather_weights([self_key], [True], gather_order[1], bits)
    (w_value,), wit_b = gather_weights([self_value], [True], gather_order[2], bits)
    (w_out,), _ = gather_weights([self_out], [True], gather_order[0], bits)
    (c_key, c_value), wit_c = gather_weights(
        [cross_key, cross_value], [True, True], gather_order[1], bits, wit_a
    )
    (c_query, c_out), wit_d = gather_weights(
        [cross_query, cross_out], [True, True], gather_order[2], bits, wit_b
    )
    (w_gate,), _ = gather_weights([ff_gate], [True], gather_order[0], bits, wit_b)
    (w_up,), _ = gather_weights([ff_up], [True], gather_order[1], bits, wit_c)
    (w_down,), _ = gather_weights([ff_down], [True], gather_order[2], bits, wit_d)
    pick = (
        lax.broadcasted_iota(jnp.int32, (8, TB), 0) == lax.broadcasted_iota(jnp.int32, (8, TB), 1)
    ).astype(bf16)
    gain_rows = nt(pick, gains)
    gain_s, gain_c, gain_f = gain_rows[0:1], gain_rows[1:2], gain_rows[2:3]

    token_all = nn(jnp.concatenate((tokens, swap(tokens, "x"))), shuffle).astype(bf16)
    enc_own = encoded.reshape(-1, width)
    states = nn(jnp.concatenate((enc_own, swap(enc_own, "x"))), shuffle).astype(bf16)
    d_branch = nn(cotangent, shuffle).astype(bf16)

    segment = segments[0]
    group_rows = segment.shape[0]
    position = jnp.arange(group_rows, dtype=jnp.int32)
    begins = jnp.sum((segment[None, :] < segment[:, None]).astype(jnp.int32), axis=1)
    base = tensor_at.astype(jnp.int32) * rows
    own_begin = lax.dynamic_slice_in_dim(begins, base, rows)
    own_segment = lax.dynamic_slice_in_dim(segment, base, rows)
    place = jnp.arange(rows, dtype=jnp.int32)
    peer_high = jnp.where(tensor_at == 1, rows - 1, -1).astype(jnp.int32)
    zero_row = jnp.zeros_like(place)
    rows_in = jnp.stack(
        (own_begin - base, place, own_begin - (rows - base), zero_row + peer_high)
        + (zero_row,) * 4
    )
    seg_in = jnp.broadcast_to(own_segment[None, :], (8, rows))
    wide = group_rows + TB
    bucket_of = jnp.pad(rel_buckets, (0, group_rows - span), mode="edge")
    chosen = (bucket_of[:, None] == jnp.arange(bucket_count)[None, :]).astype(f32)
    table = jnp.concatenate((rel_table, swap(rel_table, "x")), axis=1)
    bias = lax.dot_general(
        table, chosen, (((0,), (1,)), ((), ())), precision=exact, preferred_element_type=f32
    )
    bias = jnp.pad(bias, ((0, 0), (TB, 0))).reshape(pairs, -1, wide)
    seq_ids = jnp.arange(sequences, dtype=jnp.int32)
    blocks_of = own_segment.reshape(-1, QB)
    active = jnp.any(blocks_of[None] == seq_ids[:, None, None], axis=2).astype(jnp.int32)
    enc_base = tensor_at.astype(jnp.int32) * enc_half
    flags = jnp.concatenate(
        (
            (enc_lengths - enc_base)[:, None],
            (enc_lengths - (enc_half - enc_base))[:, None],
            active,
        ),
        axis=1,
    ).astype(jnp.int32)

    inputs_all = token_all.astype(f32)
    normed_all, scale_all, rows_one = normalize(inputs_all, gain_s)
    inputs, normed_one, scale_one = inputs_all[:rows], normed_all[:rows], scale_all[:rows]
    own_one = rows_one[:rows]
    query_s = nn(own_one, w_query).astype(bf16)
    key_s = nn(rows_one, w_key).astype(bf16)
    value_s = nn(rows_one, w_value).astype(bf16)
    attended, lse_s = self_forward(size, rows_in, bias, query_s, key_s, value_s)
    hidden_one = inputs + nt(attended, w_out)
    normed_two, scale_two, rows_two = normalize(hidden_one, gain_c)
    key_c = nn(states, c_key).astype(bf16)
    value_c = nn(states, c_value).astype(bf16)
    query_c = nn(rows_two, c_query).astype(bf16)
    crossed, lse_c = cross_forward(size, flags, seg_in, query_c, key_c, value_c)
    hidden_two = hidden_one + nt(crossed, c_out)
    normed_three, scale_three, rows_three = normalize(hidden_two, gain_f)
    gate_part = nn(rows_three, w_gate).astype(bf16)
    up_part = nn(rows_three, w_up).astype(bf16)
    activated, gelu_pull = jax.vjp(
        lambda gate_in: jax.nn.gelu(gate_in, approximate=True), gate_part.astype(f32)
    )
    up_float = up_part.astype(f32)
    hidden = (activated * up_float).astype(bf16)
    output = restore(hidden_two + nt(hidden, w_down))

    d_hidden = nn(d_branch, w_down)
    (d_gate,) = gelu_pull(d_hidden * up_float)
    d_gate = d_gate.astype(bf16)
    d_up = (d_hidden * activated).astype(bf16)
    (g_down,) = scatter_grads([split_tn(d_branch, hidden)], near_first[2], bits, piece)
    (g_gate,) = scatter_grads([split_tn(rows_three, d_gate)], near_first[0], bits, piece)
    (g_up,) = scatter_grads([split_tn(rows_three, d_up)], near_first[1], bits, piece)
    d_normed_three = nt(d_gate, w_gate) + nt(d_up, w_up)
    d_through, d_gain_f = norm_back(d_normed_three, normed_three, scale_three, gain_f)
    d_hidden_two = d_branch.astype(f32) + d_through

    d_branch_two = d_hidden_two.astype(bf16)
    d_crossed = nn(d_branch_two, c_out).astype(bf16)
    d_query_c, d_key_c, d_value_c = cross_backward(
        size, flags, seg_in, query_c, key_c, value_c, crossed, d_crossed, lse_c
    )
    g_c_out, g_c_query = scatter_grads(
        [split_tn(d_branch_two, crossed), split_tn(rows_two, d_query_c)], near_first[0], bits, piece
    )
    g_c_key, g_c_value = scatter_grads(
        [split_tn(states, d_key_c), split_tn(states, d_value_c)], near_first[1], bits, piece
    )
    d_normed_two = nt(d_query_c, c_query)
    d_through_two, d_gain_c = norm_back(d_normed_two, normed_two, scale_two, gain_c)
    d_hidden_one = d_hidden_two + d_through_two
    d_states = nt(d_key_c, c_key) + nt(d_value_c, c_value)
    enc_rows = enc_own.shape[0]
    d_states_own = d_states[:enc_rows] + swap(d_states[enc_rows:].astype(bf16), "x").astype(f32)
    grad_encoded = restore(d_states_own).reshape(encoded.shape)

    d_branch_one = d_hidden_one.astype(bf16)
    d_attended = nn(d_branch_one, w_out).astype(bf16)
    d_query_s, d_key_s, d_value_s, diagonals = self_backward(
        size, rows_in, bias, query_s, key_s, value_s, attended, d_attended, lse_s
    )
    (g_s_out,) = scatter_grads([split_tn(d_branch_one, attended)], near_first[2], bits, piece)
    d_normed_one = (
        nt(d_key_s[rows:], w_key) + nt(d_value_s[rows:], w_value)
    ).astype(bf16)
    d_normed_own = (
        nt(d_query_s, w_query) + nt(d_key_s[:rows], w_key) + nt(d_value_s[:rows], w_value)
    ) + swap(d_normed_one, "x").astype(f32)
    d_through_one, d_gain_s = norm_back(d_normed_own, normed_one, scale_one, gain_s)
    grad_tokens = restore(d_hidden_one + d_through_one)

    by_distance = jnp.roll(diagonals[:, : heads // pairs].reshape(heads, wide), 1 - 2 * TB, axis=1)
    d_table = lax.dot_general(
        chosen, by_distance[:, :group_rows], (((0,), (1,)), ((), ())),
        precision=exact, preferred_element_type=f32,
    )
    d_gains = jnp.concatenate((d_gain_s, d_gain_c, d_gain_f) + (jnp.zeros_like(d_gain_s),) * 5)
    gain_back = tn(d_gains, pick.astype(f32), exact)
    cells = bucket_count * head_local
    per_row = -(-cells // piece)

    def small_columns(part):
        flat = jnp.pad(part.reshape(-1), (0, per_row * piece - cells)).reshape(piece, per_row)
        tiled = jnp.tile(flat, (count, 1))
        return gain_back + jnp.pad(tiled, ((0, 0), (8, TB - 8 - per_row)))

    small = jnp.concatenate(
        (small_columns(d_table[:, :head_local]), small_columns(d_table[:, head_local:])), axis=1
    ).astype(bf16)
    half = width // 2
    g_s_query, g_small = scatter_grads(
        [split_tn(own_one, d_query_s), (small[:half], small[half:])], near_first[0], bits, piece
    )
    (g_s_key,) = scatter_grads([split_tn(rows_one, d_key_s)], near_first[1], bits, piece)
    (g_s_value,) = scatter_grads([split_tn(rows_one, d_value_s)], near_first[2], bits, piece)
    grad_table = g_small[:, 8 : 8 + per_row].reshape(-1)[:cells].reshape(bucket_count, head_local)
    return (
        output,
        grad_tokens,
        grad_encoded,
        g_small[:, 0],
        g_s_query,
        g_s_key,
        g_s_value,
        g_s_out,
        grad_table,
        g_small[:, 1],
        g_c_query,
        g_c_key,
        g_c_value,
        g_c_out,
        g_small[:, 2],
        g_gate,
        g_up,
        g_down,
    )


def solution(mesh):
    in_specs = (
        P(("dp", "tensor"), None),
        P("dp", "tensor", None),
        P(("dp", "tensor"), None),
        P("dp", None),
        P("dp"),
        P(),
        P("dp"),
        P("dp", "tensor"),
        P("dp", "tensor"),
        P("dp", "tensor"),
        P("dp", "tensor"),
        P(None, "tensor"),
        P("dp"),
        P("dp", "tensor"),
        P("dp", "tensor"),
        P("dp", "tensor"),
        P("dp", "tensor"),
        P("dp"),
        P("dp", "tensor"),
        P("dp", "tensor"),
        P("dp", "tensor"),
    )
    out_specs = (
        P(("dp", "tensor"), None),
        P(("dp", "tensor"), None),
        P("dp", "tensor", None),
        P("dp"),
        P("dp", "tensor"),
        P("dp", "tensor"),
        P("dp", "tensor"),
        P("dp", "tensor"),
        P(None, "tensor"),
        P("dp"),
        P("dp", "tensor"),
        P("dp", "tensor"),
        P("dp", "tensor"),
        P("dp", "tensor"),
        P("dp"),
        P("dp", "tensor"),
        P("dp", "tensor"),
        P("dp", "tensor"),
    )
    return jax.shard_map(local, mesh=mesh, in_specs=in_specs, out_specs=out_specs, check_vma=False)
```

time: 2090 us -> 644 us (0.31)
  waiting for transfers between devices: 989 us -> 245 us
  matrix products: 403 us -> 95 us
  local copies, waits for them, and re-layouts: 286 us -> 32.9 us
  blocking collectives: 238 us -> 0 us
  starting transfers between devices: 2.34 us -> 112 us
  Pallas kernels: 0 us -> 106 us
  other arithmetic: 136 us -> 39.8 us
    reduce_scatter x15 -> x0, waiting for transfers between devices: 672 us -> none  [the longest x6 163 us: sum_rows(): lax.psum_scatter(partial_rows, 'tensor', scatter_dimension=0, tiled=True)]
    dot_general x53 -> x59, matrix products: 403 us -> 95 us  [the longest x20 38.7 us: nt(): lax.dot_general(left, right, (((1,), (1,)), ((), ())), preferred_element_...]
    ppermute x0 -> x121, waiting for transfers between devices: none -> 245 us  [the longest x98 182 us: swap(): return lax.ppermute(value, 'dp', [(i, i ^ 1 << step) for i in range(count)])]
    all_gather x10 -> x0, waiting for transfers between devices: 190 us -> none  [the longest x6 116 us: gather_rows(): return lax.all_gather(own_part, 'tensor', axis=0, tiled=True)]
    and x2 -> x0, local copies, waits for them, and re-layouts: 180 us -> none  [bucket_block(): (distance[None] >= lower_edge[:, None, None]) & (distance[None] < upper_e...]
    all_gather x8 -> x0, blocking collectives: 161 us -> none  [the longest x2 43.6 us: fetch_attention(): lax.all_gather(fourth_w, 'dp', axis=0, tiled=True)]
    unnamed x31 -> x0, waiting for transfers between devices: 127 us -> none
    ppermute x0 -> x121, starting transfers between devices: none -> 112 us  [the longest x98 86 us: swap(): return lax.ppermute(value, 'dp', [(i, i ^ 1 << step) for i in range(count)])]
  transfers between devices with their start and end apart: 28 -> 121, of which waited for: 22 -> 54; matrix products, arithmetic and copies ran while one was open for 25% -> 17% of each run, Pallas kernels for 0% -> 6%
where the time goes in v1:
time: 644 us; the launch traced here: 634 us
  waiting for transfers between devices  245 us (38%)
  starting transfers between devices  112 us (17%)
  Pallas kernels  106 us (16%)
  matrix products  95 us (15%)
  other arithmetic  39.8 us (6%)
  local copies, waits for them, and re-layouts  32.9 us (5%)
    ppermute x98, waiting for transfers between devices, swap(): return lax.ppermute(value, 'dp', [(i, i ^ 1 << step) for i in range(count)])  182 us
    ppermute x98, starting transfers between devices, swap(): return lax.ppermute(value, 'dp', [(i, i ^ 1 << step) for i in range(count)])  86 us
    ppermute x23, waiting for transfers between devices, swap(): return lax.ppermute(value, 'tensor', [(0, 1), (1, 0)])  63.2 us
    dot_general x20, matrix products, nt(): lax.dot_general(left, right, (((1,), (1,)), ((), ())), preferred_element_...  38.7 us
    pallas_call x1, Pallas kernels, cross_backward(): pl.pallas_call(functools.partial(cross_backward_kernel, size), name='cros...  34.4 us
    pallas_call x1, Pallas kernels, self_backward(): pl.pallas_call(functools.partial(self_backward_kernel, size), name='self_...  30.5 us
    dot_general x23, matrix products, tn(): lax.dot_general(left, right, (((0,), (0,)), ((), ())), preferred_element_...  27.9 us
    dot_general x14, matrix products, nn(): return jnp.dot(left, right, preferred_element_type=f32)  27.6 us
  transfers between devices with their start and end apart: 121, of which 54 were waited for; matrix products, arithmetic and copies ran while one was open for 17% of the time, Pallas kernels for 6%

profile of v1, /device:TPU:0, one launch (start us, length us, event | category | flops | bytes accessed | tf_op | source)
XLA Modules:
  0.0 634.1 jit_solution(15931844996409352743)
XLA Ops:
  0.7 3.0 collective-permute-start.1
  30.0 36.4 %collective-permute-done.14 = bf16[96,384]{1,0:T(8,128)(2,1)S(1)} collective-permute-done((bf16[96,384]{1,0:T(8,128)(2,1)S(1)}, bf16[96,384]{1,0:T(8,128)(2,1)S(1)}, u32[]{:S(2)}, u32[]{:S(2)}) %collective-permute-start.14) | collective-permute-done | bytes 73760 | tf_op jit(solution)/shard_map/ppermute | solution.py:382
  73.0 3.5 collective-permute-done.10
  78.6 5.7 collective-permute-done.4
  89.7 6.6 %collective-permute-done.16 = bf16[192,768]{1,0:T(8,128)(2,1)S(1)} collective-permute-done((bf16[192,768]{1,0:T(8,128)(2,1)S(1)}, bf16[192,768]{1,0:T(8,128)(2,1)S(1)}, u32[]{:S(2)}, u32[]{:S(2)}) %collective-permute-start.16) | collective-permute-done | bytes 294944 | tf_op jit(solution)/shard_map/ppermute | solution.py:384
  97.6 3.8 collective-permute-done.23
  103.0 4.9 collective-permute-done.41
  108.5 6.9 %collective-permute-done.34 = bf16[48,768]{1,0:T(8,128)(2,1)S(1)} collective-permute-done((bf16[48,768]{1,0:T(8,128)(2,1)S(1)}, bf16[48,768]{1,0:T(8,128)(2,1)S(1)}, u32[]{:S(2)}, u32[]{:S(2)}) %collective-permute-start.34) | collective-permute-done | bytes 73760 | tf_op jit(solution)/shard_map/ppermute | solution.py:384
  115.5 5.3 collective-permute-done.30
  122.6 3.3 collective-permute-done.24
  136.5 5.1 collective-permute-done.25
  143.8 4.5 collective-permute-done.36
  161.0 4.8 collective-permute-done.26
  173.7 16.1 %self_forward.1 = (bf16[512,768]{1,0:T(8,128)(2,1)S(1)}, f32[6,8,512]{2,1,0:T(8,128)S(1)}) custom-call(s32[8,512]{1,0:T(8,128)S(1)} %stack.32.rows_ref, f32[6,2,1152]{2,1,0:T(2,128)S(1)} %reshape.685.bias_ref, bf16[512,768]{1,0:T(8,128)(2,1)S(1)} %convolution_convert_fusion.17.q_ref, bf16[1024,768]{1,0:T(8,128)(2,1)S(1)} %convolution_convert_fusion.12.k_ref, ...), custom_call_target="tpu_custom_call" | custom-call | flops 3221225472 | bytes 9437184 | tf_op jit(solution)/shard_map/self_forward/pallas_call | solution.py:289
  194.0 4.3 collective-permute-done.52
  203.3 3.4 convolution_convert_fusion.v_ref
  215.4 10.5 %collective-permute-done.53 = bf16[96,2048]{1,0:T(8,128)(2,1)S(1)} collective-permute-done((bf16[96,2048]{1,0:T(8,128)(2,1)S(1)}, bf16[96,2048]{1,0:T(8,128)(2,1)S(1)}, u32[]{:S(2)}, u32[]{:S(2)}) %collective-permute-start.53) | collective-permute-done | bytes 393248 | tf_op jit(solution)/shard_map/ppermute | solution.py:384
  231.3 25.1 %cross_forward.1 = (bf16[512,768]{1,0:T(8,128)(2,1)S(1)}, f32[6,8,512]{2,1,0:T(8,128)S(1)}) custom-call(s32[3,4]{1,0:T(4,128)S(1)} %pad_add_fusion.flags_ref, s32[8,512]{1,0:T(8,128)S(1)} %broadcast_in_dim.19.seg_ref, bf16[512,768]{1,0:T(8,128)(2,1)S(1)} %convolution_convert_fusion.16.q_ref, bf16[1536,768]{1,0:T(8,128)(2,1)S(1)} %convolution_convert_fusion.1.k_ref, ...), custom_call_target="tpu_custom_call" | custom-call | flops 1610612736 | bytes 6291456 | tf_op jit(solution)/shard_map/cross_forward/pallas_call | solution.py:339
  270.4 6.6 %fusion.4 = (bf16[512,2048]{1,0:T(8,128)(2,1)S(1)}, bf16[512,2048]{1,0:T(8,128)(2,1)S(1)}, bf16[512,2048]{1,0:T(8,128)(2,1)}) fusion(f32[512,2048]{1,0:T(8,128)S(1)} %fusion.210, bf16[512,2048]{1,0:T(8,128)(2,1)S(1)} %convolution_convert_fusion.3, bf16[512,768]{0,1:T(8,128)(2,1)S(1)} %multiply_convert_fusion.2, bf16[768,2048]{1,0:T(8,128)(2,1)S(1)} %bitcast.576), kind=kOutput, calls=%fused_computation.11 | convolution fusion | flops 1641021440 | bytes 16515072 | tf_op jit(solution)/shard_map/dot_general | solution.py:20
  282.5 34.4 %cross_backward.1 = (bf16[512,768]{1,0:T(8,128)(2,1)S(1)}, bf16[1536,768]{1,0:T(8,128)(2,1)S(1)}, bf16[1536,768]{1,0:T(8,128)(2,1)}) custom-call(s32[3,4]{1,0:T(4,128)S(1)} %pad_add_fusion.flags_ref, s32[8,512]{1,0:T(8,128)S(1)} %broadcast_in_dim.19.seg_ref, bf16[512,768]{1,0:T(8,128)(2,1)S(1)} %convolution_convert_fusion.16.q_ref, ...), custom_call_target="tpu_custom_call" | custom-call | flops 4026531840 | bytes 6291456 | tf_op jit(solution)/shard_map/cross_backward/pallas_call | solution.py:359
  322.4 30.5 %self_backward.1 = (bf16[512,768]{1,0:T(8,128)(2,1)S(1)}, bf16[1024,768]{1,0:T(8,128)(2,1)S(1)}, bf16[1024,768]{1,0:T(8,128)(2,1)}, f32[6,8,1152]{2,1,0:T(8,128)S(1)}) custom-call(s32[8,512]{1,0:T(8,128)S(1)} %stack.32.rows_ref, f32[6,2,1152]{2,1,0:T(2,128)S(1)} %reshape.685.bias_ref, bf16[512,768]{1,0:T(8,128)(2,1)S(1)} %convolution_convert_fusion.17.q_ref, ...), custom_call_target="tpu_custom_call" | custom-call | flops 8053063680 | bytes 9437184 | tf_op jit(solution)/shard_map/self_backward/pallas_call | solution.py:312
  360.2 3.4 convolution_convert_fusion.18
  363.5 4.3 fusion.213
  380.2 3.0 convolution_add_fusion.3
  388.8 4.8 convolution_add_fusion
  415.8 8.6 %collective-permute-done.65 = bf16[192,384]{1,0:T(8,128)(2,1)S(1)} collective-permute-done((bf16[192,384]{1,0:T(8,128)(2,1)S(1)}, bf16[192,384]{1,0:T(8,128)(2,1)S(1)}, u32[]{:S(2)}, u32[]{:S(2)}) %collective-permute-start.65) | collective-permute-done | bytes 147488 | tf_op jit(solution)/shard_map/ppermute | solution.py:384
  426.0 3.9 collective-permute-done.80
  431.3 3.6 collective-permute-done.82
  436.5 3.6 collective-permute-done.73
  441.7 3.5 collective-permute-done.68
  446.7 4.4 collective-permute-done.75
  460.8 3.1 collective-permute-done.69
  465.5 5.5 collective-permute-done.83
  471.5 5.3 collective-permute-done.76
  476.9 4.8 collective-permute-done.70
  482.2 4.1 collective-permute-done.84
  492.2 3.1 collective-permute-done.97
  496.7 5.2 collective-permute-done.71
  512.6 5.5 collective-permute-done.98
  536.3 4.1 collective-permute-done.60
  557.0 10.0 %collective-permute-done.62 = bf16[96,512]{1,0:T(8,128)(2,1)S(1)} collective-permute-done((bf16[96,512]{1,0:T(8,128)(2,1)S(1)}, bf16[96,512]{1,0:T(8,128)(2,1)S(1)}, u32[]{:S(2)}, u32[]{:S(2)}) %collective-permute-start.62) | collective-permute-done | bytes 98336 | tf_op jit(solution)/shard_map/ppermute | solution.py:384
  568.5 4.5 collective-permute-done.91
  574.5 3.7 collective-permute-done.63
  593.9 7.0 %collective-permute-done.118 = bf16[96,1024]{1,0:T(8,128)(2,1)S(1)} collective-permute-done((bf16[96,1024]{1,0:T(8,128)(2,1)S(1)}, bf16[96,1024]{1,0:T(8,128)(2,1)S(1)}, u32[]{:S(2)}, u32[]{:S(2)}) %collective-permute-start.118) | collective-permute-done | bytes 196640 | tf_op jit(solution)/shard_map/ppermute | solution.py:384
  604.1 3.0 collective-permute-start.109
  615.2 5.8 collective-permute-done.103
  621.9 5.0 collective-permute-done.104
  628.1 4.9 collective-permute-done.105
  (680 shorter events, 278.2 us)
Async XLA Ops:
  0.7 20.7 %collective-permute-start.1 = (f32[32,6]{0,1:T(8,128)}, f32[32,6]{0,1:T(8,128)S(1)}, u32[]{:S(2)}, u32[]{:S(2)}) collective-permute-start(f32[32,6]{0,1:T(8,128)} %param.32), channel_id=1, source_target_pairs={{0,1},{1,0},{2,3},{3,2},{4,5},{5,4},{6,7},{7,6},{8,9},{9,8},{10,11... | collective-permute-start | bytes 2312 | tf_op jit(solution)/shard_map/ppermute | solution.py:382
  3.7 19.8 %collective-permute-start.8 = (bf16[48,384]{1,0:T(8,128)(2,1)}, bf16[48,384]{1,0:T(8,128)(2,1)S(1)}, u32[]{:S(2)}, u32[]{:S(2)}) collective-permute-start(bf16[48,384]{1,0:T(8,128)(2,1)} %param.29), channel_id=1, source_target_pairs={{0,1},{1,0},{2,3},{3,2},{4,5},{5,4},{6,7},{7,6},{8,9},{9,8},{10,11... | collective-permute-start | bytes 110600 | tf_op jit(solution)/shard_map/ppermute | solution.py:382
  3.8 23.0 %collective-permute-start.13 = (bf16[48,384]{1,0:T(8,128)(2,1)}, bf16[48,384]{1,0:T(8,128)(2,1)S(1)}, u32[]{:S(2)}, u32[]{:S(2)}) collective-permute-start(bf16[48,384]{1,0:T(8,128)(2,1)} %param.30), channel_id=1, source_target_pairs={{0,4},{2,6},{4,0},{6,2},{8,12},{10,14},{12,8},{14,10},{16,20},{18,... | collective-permute-start | bytes 110600 | tf_op jit(solution)/shard_map/ppermute | solution.py:384
  5.7 18.3 %collective-permute-start.18 = (bf16[48,384]{1,0:T(8,128)(2,1)}, bf16[48,384]{1,0:T(8,128)(2,1)S(1)}, u32[]{:S(2)}, u32[]{:S(2)}) collective-permute-start(bf16[48,384]{1,0:T(8,128)(2,1)} %param.31), channel_id=1, source_target_pairs={{0,16},{2,18},{4,20},{6,22},{8,24},{10,26},{12,28},{14,30},{16,0},... | collective-permute-start | bytes 110600 | tf_op jit(solution)/shard_map/ppermute | solution.py:384
  9.9 18.5 %collective-permute-start.2 = (bf16[48,512]{1,0:T(8,128)(2,1)S(1)}, bf16[48,512]{1,0:T(8,128)(2,1)S(1)}, u32[]{:S(2)}, u32[]{:S(2)}) collective-permute-start(bf16[48,512]{1,0:T(8,128)(2,1)S(1)} %get-tuple-element.202), channel_id=1, source_target_pairs={{0,16},{2,18},{4,20},{6,22},{8,24},{10,26},{12,28},{14,30},{16,0},... | collective-permute-start | bytes 147464 | tf_op jit(solution)/shard_map/ppermute | solution.py:384
  21.4 104.6 %collective-permute-start = (bf16[512,768]{1,0:T(8,128)(2,1)}, bf16[512,768]{1,0:T(8,128)(2,1)}, u32[]{:S(2)}, u32[]{:S(2)}) collective-permute-start(bf16[512,768]{1,0:T(8,128)(2,1)} %param.21), channel_id=1, source_target_pairs={{0,1},{1,0},{2,3},{3,2},{4,5},{5,4},{6,7},{7,6},{8,9},{9,8},{10,11... | collective-permute-start | bytes 2359304 | tf_op jit(solution)/shard_map/ppermute | solution.py:382
  23.5 131.9 %collective-permute-start.28 = (bf16[768,768]{1,0:T(8,128)(2,1)}, bf16[768,768]{1,0:T(8,128)(2,1)S(1)}, u32[]{:S(2)}, u32[]{:S(2)}) collective-permute-start(bf16[768,768]{1,0:T(8,128)(2,1)} %bitcast.783), channel_id=1, source_target_pairs={{0,1},{1,0},{2,3},{3,2},{4,5},{5,4},{6,7},{7,6},{8,9},{9,8},{10,11... | collective-permute-start | bytes 3538952 | tf_op jit(solution)/shard_map/ppermute | solution.py:382
  24.1 43.9 %collective-permute-start.9 = (bf16[48,768]{1,0:T(8,128)(2,1)S(1)}, bf16[48,768]{1,0:T(8,128)(2,1)S(1)}, u32[]{:S(2)}, u32[]{:S(2)}) collective-permute-start(bf16[48,768]{1,0:T(8,128)(2,1)S(1)} %constant_dynamic-update-slice_fusion), channel_id=1, source_target_pairs={{0,16},{2,18},{4,20},{6,22},{8,24},{10,26},{12,28},{14,30},{16,0},... | collective-permute-start | bytes 221192 | tf_op jit(solution)/shard_map/ppermute | solution.py:384
  26.8 43.9 %collective-permute-start.19 = (bf16[96,384]{1,0:T(8,128)(2,1)S(1)}, bf16[96,384]{1,0:T(8,128)(2,1)S(1)}, u32[]{:S(2)}, u32[]{:S(2)}) collective-permute-start(bf16[96,384]{1,0:T(8,128)(2,1)S(1)} %bitcast.727), channel_id=1, source_target_pairs={{0,8},{2,10},{4,12},{6,14},{8,0},{10,2},{12,4},{14,6},{16,24},{18,... | collective-permute-start | bytes 221192 | tf_op jit(solution)/shard_map/ppermute | solution.py:384
  28.4 38.0 %collective-permute-start.14 = (bf16[96,384]{1,0:T(8,128)(2,1)S(1)}, bf16[96,384]{1,0:T(8,128)(2,1)S(1)}, u32[]{:S(2)}, u32[]{:S(2)}) collective-permute-start(bf16[96,384]{1,0:T(8,128)(2,1)S(1)} %bitcast.724), channel_id=1, source_target_pairs={{0,1},{1,0},{2,3},{3,2},{4,5},{5,4},{6,7},{7,6},{8,9},{9,8},{10,11... | collective-permute-start | bytes 221192 | tf_op jit(solution)/shard_map/ppermute | solution.py:382
  68.0 17.8 %collective-permute-start.15 = (bf16[96,768]{1,0:T(8,128)(2,1)S(1)}, bf16[96,768]{1,0:T(8,128)(2,1)S(1)}, u32[]{:S(2)}, u32[]{:S(2)}) collective-permute-start(bf16[96,768]{1,0:T(8,128)(2,1)S(1)} %pad_maximum_fusion.46), channel_id=1, source_target_pairs={{0,16},{2,18},{4,20},{6,22},{8,24},{10,26},{12,28},{14,30},{16,0},... | collective-permute-start | bytes 442376 | tf_op jit(solution)/shard_map/ppermute | solution.py:384
  88.9 33.5 %collective-permute-start.6 = (bf16[384,512]{1,0:T(8,128)(2,1)S(1)}, bf16[384,512]{1,0:T(8,128)(2,1)S(1)}, u32[]{:S(2)}, u32[]{:S(2)}) collective-permute-start(bf16[384,512]{1,0:T(8,128)(2,1)S(1)} %bitcast.605), channel_id=1, source_target_pairs={{0,1},{1,0},{2,3},{3,2},{4,5},{5,4},{6,7},{7,6},{8,9},{9,8},{10,11... | collective-permute-start | bytes 1179656 | tf_op jit(solution)/shard_map/ppermute | solution.py:382
  102.9 46.9 %collective-permute-start.22 = (bf16[384,768]{1,0:T(8,128)(2,1)S(1)}, bf16[384,768]{1,0:T(8,128)(2,1)S(1)}, u32[]{:S(2)}, u32[]{:S(2)}) collective-permute-start(bf16[384,768]{1,0:T(8,128)(2,1)S(1)} %get-tuple-element.152), channel_id=1, source_target_pairs={{0,2},{2,0},{4,6},{6,4},{8,10},{10,8},{12,14},{14,12},{16,18},{18,... | collective-permute-start | bytes 1769480 | tf_op jit(solution)/shard_map/ppermute | solution.py:384
  148.3 23.8 %collective-permute-start.7 = (bf16[384,768]{1,0:T(8,128)(2,1)S(1)}, bf16[384,768]{1,0:T(8,128)(2,1)S(1)}, u32[]{:S(2)}, u32[]{:S(2)}) collective-permute-start(bf16[384,768]{1,0:T(8,128)(2,1)S(1)} %get-tuple-element.154), channel_id=1, source_target_pairs={{0,2},{2,0},{4,6},{6,4},{8,10},{10,8},{12,14},{14,12},{16,18},{18,... | collective-permute-start | bytes 1769480 | tf_op jit(solution)/shard_map/ppermute | solution.py:384
  149.8 16.9 %collective-permute-start.43 = (bf16[192,1024]{1,0:T(8,128)(2,1)S(1)}, bf16[192,1024]{1,0:T(8,128)(2,1)S(1)}, u32[]{:S(2)}, u32[]{:S(2)}) collective-permute-start(bf16[192,1024]{1,0:T(8,128)(2,1)S(1)} %bitcast.608), channel_id=1, source_target_pairs={{0,4},{2,6},{4,0},{6,2},{8,12},{10,14},{12,8},{14,10},{16,20},{18,... | collective-permute-start | bytes 1179656 | tf_op jit(solution)/shard_map/ppermute | solution.py:384
  150.2 15.5 %collective-permute-start.26 = (bf16[192,768]{1,0:T(8,128)(2,1)S(1)}, bf16[192,768]{1,0:T(8,128)(2,1)S(1)}, u32[]{:S(2)}, u32[]{:S(2)}) collective-permute-start(bf16[192,768]{1,0:T(8,128)(2,1)S(1)} %bitcast.646), channel_id=1, source_target_pairs={{0,8},{2,10},{4,12},{6,14},{8,0},{10,2},{12,4},{14,6},{16,24},{18,... | collective-permute-start | bytes 884744 | tf_op jit(solution)/shard_map/ppermute | solution.py:384
  159.9 46.8 %collective-permute-start.33 = (bf16[384,768]{1,0:T(8,128)(2,1)S(1)}, bf16[384,768]{1,0:T(8,128)(2,1)}, u32[]{:S(2)}, u32[]{:S(2)}) collective-permute-start(bf16[384,768]{1,0:T(8,128)(2,1)S(1)} %bitcast.601), channel_id=1, source_target_pairs={{0,2},{2,0},{4,6},{6,4},{8,10},{10,8},{12,14},{14,12},{16,18},{18,... | collective-permute-start | bytes 1769480 | tf_op jit(solution)/shard_map/ppermute | solution.py:384
  165.8 34.3 %collective-permute-start.37 = (bf16[384,768]{1,0:T(8,128)(2,1)}, bf16[384,768]{1,0:T(8,128)(2,1)}, u32[]{:S(2)}, u32[]{:S(2)}) collective-permute-start(bf16[384,768]{1,0:T(8,128)(2,1)} %bitcast.96), channel_id=1, source_target_pairs={{0,2},{2,0},{4,6},{6,4},{8,10},{10,8},{12,14},{14,12},{16,18},{18,... | collective-permute-start | bytes 1769480 | tf_op jit(solution)/shard_map/ppermute | solution.py:384
  166.7 43.9 %collective-permute-start.27 = (bf16[384,768]{1,0:T(8,128)(2,1)}, bf16[384,768]{1,0:T(8,128)(2,1)}, u32[]{:S(2)}, u32[]{:S(2)}) collective-permute-start(bf16[384,768]{1,0:T(8,128)(2,1)} %bitcast.71), channel_id=1, source_target_pairs={{0,2},{2,0},{4,6},{6,4},{8,10},{10,8},{12,14},{14,12},{16,18},{18,... | collective-permute-start | bytes 1769480 | tf_op jit(solution)/shard_map/ppermute | solution.py:384
  172.1 84.3 %collective-permute-start.40 = (bf16[384,768]{1,0:T(8,128)(2,1)}, bf16[384,768]{1,0:T(8,128)(2,1)}, u32[]{:S(2)}, u32[]{:S(2)}) collective-permute-start(bf16[384,768]{1,0:T(8,128)(2,1)} %bitcast.105), channel_id=1, source_target_pairs={{0,2},{2,0},{4,6},{6,4},{8,10},{10,8},{12,14},{14,12},{16,18},{18,... | collective-permute-start | bytes 1769480 | tf_op jit(solution)/shard_map/ppermute | solution.py:384
  172.1 18.8 %collective-permute-start.47 = (bf16[48,2048]{1,0:T(8,128)(2,1)}, bf16[48,2048]{1,0:T(8,128)(2,1)S(1)}, u32[]{:S(2)}, u32[]{:S(2)}) collective-permute-start(bf16[48,2048]{1,0:T(8,128)(2,1)} %constant_dynamic-update-slice_fusion.2), channel_id=1, source_target_pairs={{0,16},{2,18},{4,20},{6,22},{8,24},{10,26},{12,28},{14,30},{16,0},... | collective-permute-start | bytes 589832 | tf_op jit(solution)/shard_map/ppermute | solution.py:384
  198.3 27.7 %collective-permute-start.44 = (bf16[384,1024]{1,0:T(8,128)(2,1)S(1)}, bf16[384,1024]{1,0:T(8,128)(2,1)S(1)}, u32[]{:S(2)}, u32[]{:S(2)}) collective-permute-start(bf16[384,1024]{1,0:T(8,128)(2,1)S(1)} %bitcast.574), channel_id=1, source_target_pairs={{0,1},{1,0},{2,3},{3,2},{4,5},{5,4},{6,7},{7,6},{8,9},{9,8},{10,11... | collective-permute-start | bytes 2359304 | tf_op jit(solution)/shard_map/ppermute | solution.py:382
  206.7 19.2 %collective-permute-start.53 = (bf16[96,2048]{1,0:T(8,128)(2,1)S(1)}, bf16[96,2048]{1,0:T(8,128)(2,1)S(1)}, u32[]{:S(2)}, u32[]{:S(2)}) collective-permute-start(bf16[96,2048]{1,0:T(8,128)(2,1)S(1)} %pad_maximum_fusion.31), channel_id=1, source_target_pairs={{0,16},{2,18},{4,20},{6,22},{8,24},{10,26},{12,28},{14,30},{16,0},... | collective-permute-start | bytes 1179656 | tf_op jit(solution)/shard_map/ppermute | solution.py:384
  212.9 18.1 %collective-permute-start.49 = (bf16[192,2048]{1,0:T(8,128)(2,1)S(1)}, bf16[192,2048]{1,0:T(8,128)(2,1)S(1)}, u32[]{:S(2)}, u32[]{:S(2)}) collective-permute-start(bf16[192,2048]{1,0:T(8,128)(2,1)S(1)} %bitcast.580), channel_id=1, source_target_pairs={{0,4},{2,6},{4,0},{6,2},{8,12},{10,14},{12,8},{14,10},{16,20},{18,... | collective-permute-start | bytes 2359304 | tf_op jit(solution)/shard_map/ppermute | solution.py:384
  226.0 32.9 %collective-permute-start.54 = (bf16[192,2048]{1,0:T(8,128)(2,1)S(1)}, bf16[192,2048]{1,0:T(8,128)(2,1)S(1)}, u32[]{:S(2)}, u32[]{:S(2)}) collective-permute-start(bf16[192,2048]{1,0:T(8,128)(2,1)S(1)} %bitcast.578), channel_id=1, source_target_pairs={{0,8},{2,10},{4,12},{6,14},{8,0},{10,2},{12,4},{14,6},{16,24},{18,... | collective-permute-start | bytes 2359304 | tf_op jit(solution)/shard_map/ppermute | solution.py:384
  228.1 33.4 %collective-permute-start.45 = (bf16[384,2048]{1,0:T(8,128)(2,1)}, bf16[384,2048]{1,0:T(8,128)(2,1)}, u32[]{:S(2)}, u32[]{:S(2)}) collective-permute-start(bf16[384,2048]{1,0:T(8,128)(2,1)} %get-tuple-element.130), channel_id=1, source_target_pairs={{0,2},{2,0},{4,6},{6,4},{8,10},{10,8},{12,14},{14,12},{16,18},{18,... | collective-permute-start | bytes 4718600 | tf_op jit(solution)/shard_map/ppermute | solution.py:384
  231.2 33.4 %collective-permute-start.50 = (bf16[384,2048]{1,0:T(8,128)(2,1)S(1)}, bf16[384,2048]{1,0:T(8,128)(2,1)}, u32[]{:S(2)}, u32[]{:S(2)}) collective-permute-start(bf16[384,2048]{1,0:T(8,128)(2,1)S(1)} %bitcast.563), channel_id=1, source_target_pairs={{0,2},{2,0},{4,6},{6,4},{8,10},{10,8},{12,14},{14,12},{16,18},{18,... | collective-permute-start | bytes 4718600 | tf_op jit(solution)/shard_map/ppermute | solution.py:384
  387.6 21.4 %collective-permute-start.86 = (bf16[384,768]{1,0:T(8,128)(2,1)S(1)}, bf16[384,768]{1,0:T(8,128)(2,1)S(1)}, u32[]{:S(2)}, u32[]{:S(2)}) collective-permute-start(bf16[384,768]{1,0:T(8,128)(2,1)S(1)} %copy-done.79), channel_id=1, source_target_pairs={{0,2},{2,0},{4,6},{6,4},{8,10},{10,8},{12,14},{14,12},{16,18},{18,... | collective-permute-start | bytes 1769480 | tf_op jit(solution)/shard_map/ppermute | solution.py:384
  387.7 14.7 %collective-permute-start.93 = (bf16[384,768]{1,0:T(8,128)(2,1)S(1)}, bf16[384,768]{1,0:T(8,128)(2,1)S(1)}, u32[]{:S(2)}, u32[]{:S(2)}) collective-permute-start(bf16[384,768]{1,0:T(8,128)(2,1)S(1)} %copy-done.62), channel_id=1, source_target_pairs={{0,2},{2,0},{4,6},{6,4},{8,10},{10,8},{12,14},{14,12},{16,18},{18,... | collective-permute-start | bytes 1769480 | tf_op jit(solution)/shard_map/ppermute | solution.py:384
  388.1 16.0 %collective-permute-start.92 = (bf16[384,768]{1,0:T(8,128)(2,1)S(1)}, bf16[384,768]{1,0:T(8,128)(2,1)S(1)}, u32[]{:S(2)}, u32[]{:S(2)}) collective-permute-start(bf16[384,768]{1,0:T(8,128)(2,1)S(1)} %convolution_convert_fusion.20), channel_id=1, source_target_pairs={{0,2},{2,0},{4,6},{6,4},{8,10},{10,8},{12,14},{14,12},{16,18},{18,... | collective-permute-start | bytes 1769480 | tf_op jit(solution)/shard_map/ppermute | solution.py:384
  388.2 23.6 %collective-permute-start.87 = (bf16[384,768]{1,0:T(8,128)(2,1)S(1)}, bf16[384,768]{1,0:T(8,128)(2,1)S(1)}, u32[]{:S(2)}, u32[]{:S(2)}) collective-permute-start(bf16[384,768]{1,0:T(8,128)(2,1)S(1)} %copy-done.77), channel_id=1, source_target_pairs={{0,2},{2,0},{4,6},{6,4},{8,10},{10,8},{12,14},{14,12},{16,18},{18,... | collective-permute-start | bytes 1769480 | tf_op jit(solution)/shard_map/ppermute | solution.py:384
  388.7 16.8 %collective-permute-start.79 = (bf16[384,768]{1,0:T(8,128)(2,1)S(1)}, bf16[384,768]{1,0:T(8,128)(2,1)S(1)}, u32[]{:S(2)}, u32[]{:S(2)}) collective-permute-start(bf16[384,768]{1,0:T(8,128)(2,1)S(1)} %copy-done.81), channel_id=1, source_target_pairs={{0,2},{2,0},{4,6},{6,4},{8,10},{10,8},{12,14},{14,12},{16,18},{18,... | collective-permute-start | bytes 1769480 | tf_op jit(solution)/shard_map/ppermute | solution.py:384
  406.8 123.6 %collective-permute-start.57 = (bf16[768,768]{1,0:T(8,128)(2,1)S(1)}, bf16[768,768]{1,0:T(8,128)(2,1)S(1)}, u32[]{:S(2)}, u32[]{:S(2)}) collective-permute-start(bf16[768,768]{1,0:T(8,128)(2,1)S(1)} %slice.1062), channel_id=1, source_target_pairs={{0,1},{1,0},{2,3},{3,2},{4,5},{5,4},{6,7},{7,6},{8,9},{9,8},{10,11... | collective-permute-start | bytes 3538952 | tf_op jit(solution)/shard_map/ppermute | solution.py:382
  409.0 44.0 %collective-permute-start.56 = (bf16[512,768]{0,1:T(8,128)(2,1)S(1)}, bf16[512,768]{0,1:T(8,128)(2,1)S(1)}, u32[]{:S(2)}, u32[]{:S(2)}) collective-permute-start(bf16[512,768]{0,1:T(8,128)(2,1)S(1)} %add_convert_fusion.4), channel_id=1, source_target_pairs={{0,1},{1,0},{2,3},{3,2},{4,5},{5,4},{6,7},{7,6},{8,9},{9,8},{10,11... | collective-permute-start | bytes 2359304 | tf_op jit(solution)/shard_map/ppermute | solution.py:382
  410.7 132.1 %collective-permute-start.114 = (bf16[384,2048]{1,0:T(8,128)(2,1)S(1)}, bf16[384,2048]{1,0:T(8,128)(2,1)S(1)}, u32[]{:S(2)}, u32[]{:S(2)}) collective-permute-start(bf16[384,2048]{1,0:T(8,128)(2,1)S(1)} %convolution_convert_fusion.5), channel_id=1, source_target_pairs={{0,2},{2,0},{4,6},{6,4},{8,10},{10,8},{12,14},{14,12},{16,18},{18,... | collective-permute-start | bytes 4718600 | tf_op jit(solution)/shard_map/ppermute | solution.py:384
  411.8 79.8 %collective-permute-start.94 = (bf16[192,768]{1,0:T(8,128)(2,1)S(1)}, bf16[192,768]{1,0:T(8,128)(2,1)S(1)}, u32[]{:S(2)}, u32[]{:S(2)}) collective-permute-start(bf16[192,768]{1,0:T(8,128)(2,1)S(1)} %slice_bitcast_fusion.8), channel_id=1, source_target_pairs={{0,4},{2,6},{4,0},{6,2},{8,12},{10,14},{12,8},{14,10},{16,20},{18,... | collective-permute-start | bytes 884744 | tf_op jit(solution)/shard_map/ppermute | solution.py:384
  451.2 30.5 %collective-permute-start.81 = (bf16[96,384]{1,0:T(8,128)(2,1)S(1)}, bf16[96,384]{1,0:T(8,128)(2,1)S(1)}, u32[]{:S(2)}, u32[]{:S(2)}) collective-permute-start(bf16[96,384]{1,0:T(8,128)(2,1)S(1)} %bitcast.762), channel_id=1, source_target_pairs={{0,16},{2,18},{4,20},{6,22},{8,24},{10,26},{12,28},{14,30},{16,0},... | collective-permute-start | bytes 221192 | tf_op jit(solution)/shard_map/ppermute | solution.py:384
  491.5 37.4 %collective-permute-start.88 = (bf16[384,768]{1,0:T(8,128)(2,1)S(1)}, bf16[384,768]{1,0:T(8,128)(2,1)S(1)}, u32[]{:S(2)}, u32[]{:S(2)}) collective-permute-start(bf16[384,768]{1,0:T(8,128)(2,1)S(1)} %pad_maximum_fusion.25), channel_id=1, source_target_pairs={{0,1},{1,0},{2,3},{3,2},{4,5},{5,4},{6,7},{7,6},{8,9},{9,8},{10,11... | collective-permute-start | bytes 1769480 | tf_op jit(solution)/shard_map/ppermute | solution.py:382
  525.2 22.6 %collective-permute-start.106 = (bf16[384,2048]{1,0:T(8,128)(2,1)S(1)}, bf16[384,2048]{1,0:T(8,128)(2,1)S(1)}, u32[]{:S(2)}, u32[]{:S(2)}) collective-permute-start(bf16[384,2048]{1,0:T(8,128)(2,1)S(1)} %copy-done.74), channel_id=1, source_target_pairs={{0,2},{2,0},{4,6},{6,4},{8,10},{10,8},{12,14},{14,12},{16,18},{18,... | collective-permute-start | bytes 4718600 | tf_op jit(solution)/shard_map/ppermute | solution.py:384
  528.2 21.5 %collective-permute-start.101 = (bf16[384,2048]{1,0:T(8,128)(2,1)S(1)}, bf16[384,2048]{1,0:T(8,128)(2,1)S(1)}, u32[]{:S(2)}, u32[]{:S(2)}) collective-permute-start(bf16[384,2048]{1,0:T(8,128)(2,1)S(1)} %copy-done.73), channel_id=1, source_target_pairs={{0,2},{2,0},{4,6},{6,4},{8,10},{10,8},{12,14},{14,12},{16,18},{18,... | collective-permute-start | bytes 4718600 | tf_op jit(solution)/shard_map/ppermute | solution.py:384
  544.9 39.0 %collective-permute-start.115 = (bf16[192,1024]{1,0:T(8,128)(2,1)}, bf16[192,1024]{1,0:T(8,128)(2,1)}, u32[]{:S(2)}, u32[]{:S(2)}) collective-permute-start(bf16[192,1024]{1,0:T(8,128)(2,1)} %bitcast.262), channel_id=1, source_target_pairs={{0,8},{2,10},{4,12},{6,14},{8,0},{10,2},{12,4},{14,6},{16,24},{18,... | collective-permute-start | bytes 1179656 | tf_op jit(solution)/shard_map/ppermute | solution.py:384
  547.8 37.7 %collective-permute-start.117 = (bf16[192,1024]{1,0:T(8,128)(2,1)}, bf16[192,1024]{1,0:T(8,128)(2,1)}, u32[]{:S(2)}, u32[]{:S(2)}) collective-permute-start(bf16[192,1024]{1,0:T(8,128)(2,1)} %bitcast.268), channel_id=1, source_target_pairs={{0,8},{2,10},{4,12},{6,14},{8,0},{10,2},{12,4},{14,6},{16,24},{18,... | collective-permute-start | bytes 1179656 | tf_op jit(solution)/shard_map/ppermute | solution.py:384
  549.7 39.7 %collective-permute-start.107 = (bf16[192,1024]{1,0:T(8,128)(2,1)}, bf16[192,1024]{1,0:T(8,128)(2,1)}, u32[]{:S(2)}, u32[]{:S(2)}) collective-permute-start(bf16[192,1024]{1,0:T(8,128)(2,1)} %slice_bitcast_fusion.2), channel_id=1, source_target_pairs={{0,4},{2,6},{4,0},{6,2},{8,12},{10,14},{12,8},{14,10},{16,20},{18,... | collective-permute-start | bytes 1179656 | tf_op jit(solution)/shard_map/ppermute | solution.py:384
  553.3 37.4 %collective-permute-start.110 = (bf16[192,1024]{1,0:T(8,128)(2,1)}, bf16[192,1024]{1,0:T(8,128)(2,1)}, u32[]{:S(2)}, u32[]{:S(2)}) collective-permute-start(bf16[192,1024]{1,0:T(8,128)(2,1)} %slice_bitcast_fusion), channel_id=1, source_target_pairs={{0,4},{2,6},{4,0},{6,2},{8,12},{10,14},{12,8},{14,10},{16,20},{18,... | collective-permute-start | bytes 1179656 | tf_op jit(solution)/shard_map/ppermute | solution.py:384
  578.2 32.4 %collective-permute-start.102 = (bf16[384,1024]{1,0:T(8,128)(2,1)}, bf16[384,1024]{1,0:T(8,128)(2,1)}, u32[]{:S(2)}, u32[]{:S(2)}) collective-permute-start(bf16[384,1024]{1,0:T(8,128)(2,1)} %slice.806), channel_id=1, source_target_pairs={{0,1},{1,0},{2,3},{3,2},{4,5},{5,4},{6,7},{7,6},{8,9},{9,8},{10,11... | collective-permute-start | bytes 2359304 | tf_op jit(solution)/shard_map/ppermute | solution.py:382
  585.2 29.9 %collective-permute-start.116 = (bf16[96,1024]{1,0:T(8,128)(2,1)S(1)}, bf16[96,1024]{1,0:T(8,128)(2,1)S(1)}, u32[]{:S(2)}, u32[]{:S(2)}) collective-permute-start(bf16[96,1024]{1,0:T(8,128)(2,1)S(1)} %bitcast.739), channel_id=1, source_target_pairs={{0,16},{2,18},{4,20},{6,22},{8,24},{10,26},{12,28},{14,30},{16,0},... | collective-permute-start | bytes 589832 | tf_op jit(solution)/shard_map/ppermute | solution.py:384
  586.6 14.3 %collective-permute-start.118 = (bf16[96,1024]{1,0:T(8,128)(2,1)S(1)}, bf16[96,1024]{1,0:T(8,128)(2,1)S(1)}, u32[]{:S(2)}, u32[]{:S(2)}) collective-permute-start(bf16[96,1024]{1,0:T(8,128)(2,1)S(1)} %bitcast.741), channel_id=1, source_target_pairs={{0,16},{2,18},{4,20},{6,22},{8,24},{10,26},{12,28},{14,30},{16,0},... | collective-permute-start | bytes 589832 | tf_op jit(solution)/shard_map/ppermute | solution.py:384
  600.9 14.1 %collective-permute-start.119 = (bf16[96,1024]{1,0:T(8,128)(2,1)S(1)}, bf16[96,1024]{1,0:T(8,128)(2,1)S(1)}, u32[]{:S(2)}, u32[]{:S(2)}) collective-permute-start(bf16[96,1024]{1,0:T(8,128)(2,1)S(1)} %fusion.99), channel_id=1, source_target_pairs={{0,1},{1,0},{2,3},{3,2},{4,5},{5,4},{6,7},{7,6},{8,9},{9,8},{10,11... | collective-permute-start | bytes 589832 | tf_op jit(solution)/shard_map/ppermute | solution.py:382
  (167 other events, 1486.2 us)
